TPU v7x, 128 devices: a whole 4x4x4 slice. The times are simulated.
128 devices in a mesh: lat: 32 (over y, x, core), lev: 4 (over z).
Axes of the slice: x: 4, y: 4, z: 4, core: 2. Of those that a mesh axis runs over, the one named last changes fastest.
Arguments:
- adjoint_grid: bfloat16 [32, 64, 2, 5136], P('lev', 'lat'), may hold values from -6 to 6
- lower_diffusion: float32 [32, 64, 5136], P(None, 'lat', 'lev'), may hold values from 0.2 to 20
- upper_diffusion: float32 [32, 64, 5136], P(None, 'lat', 'lev'), may hold values from 0.2 to 20
- row_lengths: int32 [32], replicated, may hold values from 1280 to 5136, as said below
- wave_order: int32 [1280], replicated, may hold values from 0 to 1279, each once
Outputs:
- spectral: float32 [1280, 2, 2, 32, 64], P('lat', None, None, 'lev')
Inputs may be any that keep to these rules, and one draw needn't show every extreme that they name: `row_lengths`: lengths never fall from pole to equator; the first is 1280 and the last 5136.
All inputs are finite; a program needn't handle non-finite values.
Results may differ from a plain program's by a relative error of at most 0.0037.
Values may be sent and summed in bfloat16 or wider, within the bound.
No kernel may reach another device: no remote copies, remote signals or barrier semaphores. Data moves between devices by JAX's collectives and lax.ppermute only.
A program may use at most 128 MiB of HBM per device.

v0:
```python
import jax
import jax.numpy as jnp
from jax import lax
from jax.sharding import PartitionSpec as P

MW = 1280


TWO_PI = 6.283185307179586


def from_partner(block, axis, distance):
    count = lax.axis_size(axis)
    route = []
    for low in range(count):
        high = low | 1 << distance
        if high != low and high < count:
            route += [(low, high), (high, low)]
    return lax.ppermute(block, axis, route)


def fourier_basis(length, points, offset, wavenumbers):
    points_index = offset + lax.iota(jnp.int32, points)
    wave_index = lax.iota(jnp.int32, wavenumbers)
    product_index = points_index[:, None] * wave_index[None, :] % length
    phase_angle = TWO_PI * product_index.astype(jnp.float32) / length.astype(jnp.float32)
    inside = (points_index[:, None] < length) & (2 * wave_index[None, :] < length)
    cos_part = jnp.where(inside, jnp.cos(phase_angle), 0.0).astype(jnp.bfloat16)
    sin_part = jnp.where(inside, -jnp.sin(phase_angle), 0.0).astype(jnp.bfloat16)
    return jnp.concatenate([cos_part, sin_part], axis=1)


def vertical_adjoint(values_in, lower_diffusion, upper_diffusion):
    levels = values_in.shape[0]
    final_level = levels - 1
    ratios = []
    right_parts = []
    for level in range(levels):
        if level == 0:
            pivot = 1.0 + upper_diffusion[0]
            right_part = values_in[0] / pivot
        else:
            if level == final_level:
                diagonal_term = 1.0 + lower_diffusion[level]
            else:
                diagonal_term = 1.0 + lower_diffusion[level] + upper_diffusion[level]
            pivot = diagonal_term + upper_diffusion[level - 1] * ratios[level - 1]
            right_part = (
                values_in[level] + upper_diffusion[level - 1] * right_parts[level - 1]
            ) / pivot
        right_parts.append(right_part)
        if level < final_level:
            ratios.append(-lower_diffusion[level + 1] / pivot)
    current = right_parts[final_level]
    results = [current]
    for level in range(final_level - 1, -1, -1):
        current = right_parts[level] - ratios[level] * current
        results.append(current)
    return jnp.stack(results[::-1])


def spectra_of(portion, lengths, offset):
    points = portion.shape[3]
    rows_first = jnp.transpose(portion, (1, 0, 2, 3))

    def one_row(member):
        source, length = member
        basis = fourier_basis(length, points, offset, MW)
        flattened = source.reshape(source.shape[0] * source.shape[1], points)
        product = jnp.dot(flattened, basis, preferred_element_type=jnp.float32)
        product = product / jnp.sqrt(length.astype(jnp.float32))
        return product.reshape(source.shape[0], source.shape[1], 2, MW)

    results = lax.map(one_row, (rows_first, lengths))
    return jnp.transpose(results, (1, 0, 2, 3, 4))


def body(adjoint_grid, lower_diffusion, upper_diffusion, row_lengths, wave_order):
    lat_count = lax.axis_size("lat")
    half_count = lat_count // 2
    mirror_bit = lat_count.bit_length() - 2
    position = lax.axis_index("lat")
    row_count = adjoint_grid.shape[1]
    first_pair = position % half_count * row_count
    lengths = lax.dynamic_slice_in_dim(row_lengths, first_pair, row_count, 0)
    northern = position < half_count
    columns = lax.all_to_all(adjoint_grid, "lev", split_axis=3, concat_axis=0, tiled=True)
    solved = vertical_adjoint(
        columns.astype(jnp.float32), lower_diffusion[:, :, None, :], upper_diffusion[:, :, None, :]
    ).astype(jnp.bfloat16)
    level_rows = lax.all_to_all(solved, "lev", split_axis=0, concat_axis=3, tiled=True)
    spectra = spectra_of(level_rows, lengths, 0)
    partner = from_partner(spectra, "lat", mirror_bit)
    spectra = jnp.where(northern, spectra + partner, partner - spectra)
    ordered = jnp.take(spectra, wave_order, axis=4)
    by_wave = jnp.transpose(ordered, (4, 3, 2, 0, 1))
    spectral = lax.all_to_all(by_wave, "lat", split_axis=0, concat_axis=4, tiled=True)
    return spectral


def solution(mesh):
    in_specs = (P("lev", "lat", None, None), P(None, "lat", "lev"), P(None, "lat", "lev"), P(), P())
    out_specs = P("lat", None, None, "lev", None)
    return jax.shard_map(body, mesh=mesh, in_specs=in_specs, out_specs=out_specs, check_vma=False)
```

profile of v0, /device:TPU:1, one launch (start us, length us, event | category | flops | bytes accessed | tf_op | source)
XLA Modules:
  0.0 905.4 jit_solution(15454656203606970228)
XLA Ops:
  0.0 11.6 %copy.43 = bf16[8,2,2,5136]{0,2,1,3:T(2,128)(2,1)} copy(bf16[8,2,2,5136]{3,2,1,0:T(2,128)(2,1)} %param.7) | data formatting | bytes 657408 | tf_op args[0]
  11.6 7.6 reshape.12717
  19.2 6.0 all-to-all-start
  25.2 0.9 slice_bitcast_fusion.29
  26.1 0.9 slice_bitcast_fusion.30
  27.0 1.8 bitcast_add_fusion.1
  28.8 0.7 broadcast_add_fusion
  29.5 2.0 all-to-all-done
  31.5 5.4 reshape.12718
  36.9 10.3 %copy.44 = bf16[8,2,2,5136]{3,0,2,1:T(8,128)(2,1)S(1)} copy(bf16[8,2,2,5136]{0,2,1,3:T(2,128)(2,1)} %bitcast.537) | data formatting | bytes 657408 | tf_op jit(solution)/shard_map/all_to_all | solution.py:87
  47.8 1.8 fusion.94
  50.7 1.1 stack.3
  51.8 1.0 copy.46
  52.8 3.6 all-to-all-start.1
  56.6 5.7 all-to-all-done.1
  62.8 751.5 %while.10 = (s32[]{:T(128)}, f32[2,8,2,2,1280]{4,3,2,1,0:T(2,128)S(1)}, bf16[2,8,2,5136]{3,1,2,0:T(8,128)(2,1)S(1)}, s32[2]{0:T(128)S(1)}, s32[]{:T(128)}, /*index=5*/s32[]{:T(128)}) while((s32[]{:T(128)}, f32[2,8,2,2,1280]{4,3,2,1,0:T(2,128)S(1)}, bf16[2,8,2,5136]{3,1,2,0:T(8,128)(2,1)S(1)}, s32[2]{0:T(128)S(1)}, s32[]{:T(128)}, ...), condition=%wide.region_1.2_spmd, body=%wide.region_0.1_spmd.sunk | while | flops 585141760 | bytes 54575300 | solution.py:74
  66.9 361.0 %fusion.179 = (bf16[5136,1280]{1,0:T(8,128)(2,1)}, bf16[5136,1280]{1,0:T(8,128)(2,1)}) fusion(f32[]{:T(128)S(6)} %convert_element_type.49, pred[]{:T(512)S(6)} %lt.92, s32[]{:T(128)S(6)} %select_n.84, pred[1280]{0:T(1024)(128)(4,1)S(1)} %multiply_compare_fusion.2, pred[5136]{0:T(1024)(128)(4,1)S(1)} %iota_compare_fusion.2), kind=kLoop, calls=%fused_computation.4.clone.1 | loop fusion | flops 111759360 | bytes 26302744 | tf_op jit(solution)/shard_map/while/body/eval_jaxpr/convert_element_type | solution.py:28
  428.0 10.3 %fusion.180 = f32[16,2560]{1,0:T(8,128)S(1)} fusion(bf16[16,5136]{1,0:T(8,128)(2,1)S(1)} %reshape.12722, bf16[5136,1280]{1,0:T(8,128)(2,1)} %get-tuple-element.252, bf16[5136,1280]{1,0:T(8,128)(2,1)} %get-tuple-element.253, f32[]{:T(128)S(6)} %sqrt.4), kind=kOutput, calls=%fused_computation.18.clone.1 | convolution fusion | flops 473374720 | bytes 26624516 | tf_op jit(solution)/shard_map/while/body/eval_jaxpr/dot_general | solution.py:70
  442.7 361.0 %fusion.179 = (bf16[5136,1280]{1,0:T(8,128)(2,1)}, bf16[5136,1280]{1,0:T(8,128)(2,1)}) fusion(f32[]{:T(128)S(6)} %convert_element_type.49, pred[]{:T(512)S(6)} %lt.92, s32[]{:T(128)S(6)} %select_n.84, pred[1280]{0:T(1024)(128)(4,1)S(1)} %multiply_compare_fusion.2, pred[5136]{0:T(1024)(128)(4,1)S(1)} %iota_compare_fusion.2), kind=kLoop, calls=%fused_computation.4.clone.1 | loop fusion | flops 111759360 | bytes 26302744 | tf_op jit(solution)/shard_map/while/body/eval_jaxpr/convert_element_type | solution.py:28
  803.7 10.3 %fusion.180 = f32[16,2560]{1,0:T(8,128)S(1)} fusion(bf16[16,5136]{1,0:T(8,128)(2,1)S(1)} %reshape.12722, bf16[5136,1280]{1,0:T(8,128)(2,1)} %get-tuple-element.252, bf16[5136,1280]{1,0:T(8,128)(2,1)} %get-tuple-element.253, f32[]{:T(128)S(6)} %sqrt.4), kind=kOutput, calls=%fused_computation.18.clone.1 | convolution fusion | flops 473374720 | bytes 26624516 | tf_op jit(solution)/shard_map/while/body/eval_jaxpr/dot_general | solution.py:70
  814.3 3.2 collective-permute-start
  817.6 4.7 copy.50
  822.3 4.7 copy.52
  827.0 8.9 fusion.17
  835.8 13.5 %gather_fusion = f32[1280,8,2,2,2]{1,4,3,2,0:T(2,128)} fusion(f32[8,2,2,2,1280]{0,3,4,2,1:T(2,128)} %fusion.17, s32[2048]{0:T(1024)S(1)} %pad_clamp_fusion), kind=kCustom, calls=%fused_computation | custom fusion | bytes 660480 | tf_op jit(solution)/shard_map/jit(_take)/gather | solution.py:95
  849.4 8.2 fusion.171
  857.6 8.7 reshape.12719
  866.3 20.6 %all_to_all.45 = f32[32,1,2560]{2,1,0:T(1,128)S(1)} all-to-all(f32[32,1,2560]{2,1,0:T(1,128)S(1)} %reshape.12719), channel_id=1, replica_groups=mesh['lat'=32,'lev'=4] {'lat'}, dimensions={0} | all-to-all | bytes 655360 | tf_op jit(solution)/shard_map/all_to_all | solution.py:97
  887.3 1.4 reduce
  888.8 9.5 %reshape.12720 = f32[1280,2,2,2,8]{4,3,2,1,0:T(2,128)} reshape(f32[32,2560]{1,0:T(8,128)S(1)} %reduce) | data formatting | bytes 655360
  898.3 5.6 copy.54
  903.9 1.5 copy.55
  (49 shorter events, 7.3 us)
Async XLA Ops:
  19.2 37.3 %copy-start.1 = (s32[32]{0:T(128)S(1)}, s32[32]{0:T(128)}, u32[]{:S(2)}) copy-start(s32[32]{0:T(128)} %param.10) | copy-start | bytes 388
  19.2 37.3 %copy-start = (s32[1280]{0:T(1024)S(1)}, s32[1280]{0:T(1024)}, u32[]{:S(2)}) copy-start(s32[1280]{0:T(1024)} %param.11) | copy-start | bytes 15364
  19.2 12.2 %all-to-all-start = ((bf16[4,2,20544]{2,1,0:T(2,128)(2,1)}), bf16[4,2,20544]{2,1,0:T(2,128)(2,1)S(1)}, u32[]{:S(2)}, u32[]{:S(2)}) async-start(bf16[4,2,20544]{2,1,0:T(2,128)(2,1)} %reshape.12717), calls=%async_computation | async-start | bytes 659456 | tf_op jit(solution)/shard_map/all_to_all | solution.py:87
  52.8 9.5 %all-to-all-start.1 = ((bf16[32,2,2,1284]{3,2,1,0:T(2,128)(2,1)}), bf16[32,2,2,1284]{3,2,1,0:T(2,128)(2,1)S(1)}, u32[]{:S(2)}, u32[]{:S(2)}) async-start(bf16[32,2,2,1284]{3,2,1,0:T(2,128)(2,1)} %copy.46), calls=%async_computation.1 | async-start | bytes 720896 | tf_op jit(solution)/shard_map/all_to_all | solution.py:91
  814.3 7.9 collective-permute-start
where the time goes:
time: 908 us; the launch traced here: 905 us
  other arithmetic  748 us (82%)
  local copies, waits for them, and re-layouts  90.8 us (10%)
  matrix products  20.7 us (2%)
  blocking collectives  20.6 us (2%)
  starting transfers between devices  12.8 us (1%)
    convert_element_type x2, other arithmetic, fourier_basis(): cos_part = jnp.where(inside, jnp.cos(phase_angle), 0.0).astype(jnp.bfloat16)  722 us
    unnamed x9, local copies, waits for them, and re-layouts  42.9 us
    dot_general x2, matrix products, one_row(): product = jnp.dot(flattened, basis, preferred_element_type=jnp.float32)  20.7 us
    all_to_all x1, blocking collectives, body(): lax.all_to_all(by_wave, 'lat', split_axis=0, concat_axis=4, tiled=True)  20.6 us
  transfers between devices with their start and end apart: 3, of which 2 were waited for; matrix products, arithmetic and copies ran while one was open for 1% of the time, Pallas kernels for 0%

commit v1 on v0

v1 whole, which is shorter than its diff:
```python
import jax
import jax.numpy as jnp
from jax import lax
from jax.experimental import pallas as pl
from jax.experimental.pallas import tpu as pltpu
from jax.sharding import PartitionSpec as P

LANE = 128
DEEP = 256
TWO_PI = 6.283185307179586
VMEM = pl.BlockSpec(memory_space=pltpu.VMEM)
SMEM = pl.BlockSpec(memory_space=pltpu.SMEM)


def sizes(points, lev_count):
    block = points // lev_count
    step = block // LANE * LANE
    window = step + LANE
    return block, step, window


def pack_kernel(lev_count, points, x_ref, *outs):
    block, step, window = sizes(points, lev_count)
    levels, rows, fields = x_ref.shape[:3]
    last = points - lev_count * step
    me = lax.axis_index("lev")
    for shift, out in enumerate(outs):
        to = lax.rem(me + shift, lev_count)
        base = pl.multiple_of(to * step, LANE)
        for row in range(rows):
            for level in range(levels):
                low = fields * level
                out[row, low : low + fields, :step] = x_ref[level, row, :, pl.ds(base, step)]

        @pl.when(to < lev_count - 1)
        def _():
            tail = pl.multiple_of(to * step + step, LANE)
            for row in range(rows):
                for level in range(levels):
                    low = fields * level
                    out[row, low : low + fields, step:] = x_ref[level, row, :, pl.ds(tail, LANE)]

        @pl.when(to == lev_count - 1)
        def _():
            for row in range(rows):
                for level in range(levels):
                    low = fields * level
                    out[row, low : low + fields, step : step + last] = x_ref[level, row, :, lev_count * step :]


def turn(multiple, length):
    inverse = 1.0 / length
    rest = multiple - jnp.floor(multiple * inverse) * length
    rest = jnp.where(rest < 0.0, rest + length, rest)
    rest = jnp.where(rest >= length, rest - length, rest)
    quarter = jnp.floor(4.0 * rest * inverse + 0.5)
    angle = (4.0 * rest - quarter * length) * ((TWO_PI / 4.0) * inverse)
    square = angle * angle
    sine = angle + angle * square * (-1.6666654611e-1 + square * (8.3321608736e-3 + square * -1.9515295891e-4))
    cosine = 1.0 - 0.5 * square + square * square * (
        4.166664568298827e-2 + square * (-1.388731625493765e-3 + square * 2.443315711809948e-5)
    )
    odd = (quarter == 1.0) | (quarter == 3.0)
    real = jnp.where(odd, sine, cosine)
    imag = jnp.where(odd, cosine, sine)
    real = jnp.where((quarter == 1.0) | (quarter == 2.0), -real, real)
    imag = jnp.where((quarter == 2.0) | (quarter == 3.0), imag, -imag)
    return real, imag


def prepare_kernel(
    lev_count, points, lengths_ref, wave_ref, lower_ref, upper_ref, fine_ref, coarse_ref, first_ref, second_ref, third_ref
):
    block, step, window = sizes(points, lev_count)
    rows = fine_ref.shape[0]
    waves = wave_ref.shape[1]
    halves = lengths_ref.shape[0]
    wave = wave_ref[...].astype(jnp.float32)
    me_lat = lax.axis_index("lat")
    me_lev = lax.axis_index("lev")
    coarse_rows = coarse_ref.shape[2]
    small = lax.broadcasted_iota(jnp.int32, (16, 1), 0).astype(jnp.float32)
    blocks = lax.broadcasted_iota(jnp.int32, (coarse_rows, 1), 0).astype(jnp.float32)
    for row in range(rows):
        whole = lengths_ref[lax.rem(me_lat * rows + row, halves)]
        length = jnp.full((1, 1), whole, jnp.int32).astype(jnp.float32)
        near_real, near_imag = turn(wave * small, length)
        far_real, far_imag = turn(wave * (16.0 * small), length)
        for part in range(16):
            one_real = far_real[part : part + 1]
            one_imag = far_imag[part : part + 1]
            low = 16 * part
            fine_ref[row, low : low + 16, :waves] = (near_real * one_real - near_imag * one_imag).astype(jnp.bfloat16)
            fine_ref[row, low : low + 16, waves:] = (near_real * one_imag + near_imag * one_real).astype(jnp.bfloat16)
        real, imag = turn(wave * (float(DEEP) * blocks), length)
        scale = jnp.where(2.0 * wave < length, 1.0 / jnp.sqrt(length), 0.0)
        coarse_ref[row, 0] = real * scale
        coarse_ref[row, 1] = imag * scale

    levels = lower_ref.shape[0]
    own = first_ref.shape[2] // 2
    ratio = None
    for level in range(levels):
        upper = upper_ref[level]
        if level == 0:
            pivot = 1.0 + upper
            above = jnp.zeros_like(upper)
        else:
            diagonal = 1.0 + lower_ref[level]
            if level < levels - 1:
                diagonal = diagonal + upper
            above = upper_ref[level - 1]
            pivot = diagonal + above * ratio
        inverse = 1.0 / pivot
        if level < levels - 1:
            ratio = -lower_ref[level + 1] * inverse
        else:
            ratio = jnp.zeros_like(inverse)
        chunk, inner = divmod(level, own)
        for out, value in ((first_ref, inverse), (second_ref, above * inverse), (third_ref, ratio)):
            for row in range(rows):
                out[chunk, row, 2 * inner : 2 * inner + 2, :block] = jnp.broadcast_to(value[row : row + 1], (2, block))
    for out in (first_ref, second_ref, third_ref):
        for chunk in range(out.shape[0]):
            for row in range(rows):
                out[chunk, row] = pltpu.roll(out[chunk, row], me_lev * (block - step), 1)


def solve_kernel(lev_count, points, lengths_ref, first_ref, second_ref, third_ref, *refs):
    block, step, window = sizes(points, lev_count)
    sources, outs, work = refs[:lev_count], refs[lev_count : 2 * lev_count], refs[-1]
    rows = work.shape[1]
    own = work.shape[2] // 2
    levels = lev_count * own
    halves = lengths_ref.shape[0]
    me_lat = lax.axis_index("lat")
    me_lev = lax.axis_index("lev")
    for shift, source in enumerate(sources):
        chunk = lax.rem(me_lev + lev_count - shift, lev_count)
        for row in range(rows):
            work[chunk, row] = source[row].astype(jnp.float32)
    lane = lax.broadcasted_iota(jnp.int32, (1, window), 1)
    offset = me_lev * (block - step)
    inside = []
    for row in range(rows):
        whole = lengths_ref[lax.rem(me_lat * rows + row, halves)]
        inside.append((lane >= offset) & (lane < offset + block) & (lane + me_lev * step < whole))
    for row in range(rows):
        part = None
        for level in range(levels):
            chunk, inner = divmod(level, own)
            at = (chunk, row, slice(2 * inner, 2 * inner + 2))
            value = work[at] * first_ref[at]
            part = value if part is None else value + second_ref[at] * part
            work[at] = part
        current = None
        for level in range(levels - 1, -1, -1):
            chunk, inner = divmod(level, own)
            at = (chunk, row, slice(2 * inner, 2 * inner + 2))
            current = work[at] if current is None else work[at] - third_ref[at] * current
            work[at] = current
    for shift, out in enumerate(outs):
        chunk = lax.rem(me_lev + shift, lev_count)
        for row in range(rows):
            out[row] = jnp.where(inside[row], work[chunk, row], 0.0).astype(jnp.bfloat16)


def fourier_kernel(lev_count, points, fine_ref, coarse_ref, *refs):
    block, step, window = sizes(points, lev_count)
    sources, out_ref, spectra, turned = refs[:lev_count], refs[-3], refs[-2], refs[-1]
    rows = fine_ref.shape[0]
    waves = fine_ref.shape[2] // 2
    per = step // DEEP
    me_lev = lax.axis_index("lev")
    members = sources[0].shape[1]
    for row in range(rows):
        main = jnp.concatenate(
            [source[row, :, DEEP * a : DEEP * (a + 1)] for source in sources for a in range(per)], axis=0
        )
        tail = jnp.concatenate([source[row, :, step:] for source in sources], axis=0)
        for tile in range(waves // DEEP):
            low = DEEP * tile
            cos_table = fine_ref[row, :, low : low + DEEP]
            sin_table = fine_ref[row, :, waves + low : waves + low + DEEP]
            main_cos = jnp.dot(main, cos_table, preferred_element_type=jnp.float32)
            main_sin = jnp.dot(main, sin_table, preferred_element_type=jnp.float32)
            tail_cos = jnp.dot(tail, cos_table[:LANE], preferred_element_type=jnp.float32)
            tail_sin = jnp.dot(tail, sin_table[:LANE], preferred_element_type=jnp.float32)
            real = jnp.zeros((members, DEEP), jnp.float32)
            imag = jnp.zeros((members, DEEP), jnp.float32)
            for shift in range(lev_count):
                begin = per * lax.rem(me_lev + lev_count - shift, lev_count)
                for a in range(per + 1):
                    if a < per:
                        pos = members * (per * shift + a)
                        y_cos, y_sin = main_cos[pos : pos + members], main_sin[pos : pos + members]
                    else:
                        pos = members * shift
                        y_cos, y_sin = tail_cos[pos : pos + members], tail_sin[pos : pos + members]
                    c = coarse_ref[row, 0, pl.ds(begin + a, 1), low : low + DEEP]
                    s = coarse_ref[row, 1, pl.ds(begin + a, 1), low : low + DEEP]
                    real = real + (y_cos * c - y_sin * s)
                    imag = imag + (y_sin * c + y_cos * s)
            for half in range(DEEP // LANE):
                at = tile * (DEEP // LANE) + half
                spectra[row, 0, at] = real[:, LANE * half : LANE * (half + 1)]
                spectra[row, 1, at] = imag[:, LANE * half : LANE * (half + 1)]
    for tile in range(waves // LANE):
        low = LANE * tile
        pieces = []
        for row in range(rows):
            one = [
                spectra[row, c, tile, pl.ds(field, members // 2, stride=2), :] for c in range(2) for field in range(2)
            ]
            pieces += one + one
        turned[low : low + LANE, :] = jnp.concatenate(pieces, axis=0).T
    turned[waves:, :] = jnp.zeros((turned.shape[0] - waves, LANE), jnp.float32)
    parts = out_ref.shape[0]
    high = out_ref.shape[1]
    slots = waves // parts
    lane = lax.broadcasted_iota(jnp.int32, (high, LANE), 1)
    left = lax.rem(lane, LANE // 2) < LANE // 4
    for part in range(parts):
        top = turned[slots * part : slots * part + high, :]
        low = turned[slots * part + high : slots * part + 2 * high, :]
        out_ref[part] = jnp.where(left, top, low).astype(jnp.bfloat16)


def pair_kernel(in_ref, out_ref, work):
    parts, high = in_ref.shape[:2]
    slots = out_ref.shape[0]
    grid_rows = out_ref.shape[4]
    rows = grid_rows // parts
    for part in range(parts):
        work[high * part : high * (part + 1), :] = in_ref[part].astype(jnp.float32)
    source = lax.broadcasted_iota(jnp.int32, (parts, grid_rows), 0)
    target = lax.broadcasted_iota(jnp.int32, (parts, grid_rows), 1)
    half = grid_rows // 2
    mixes = []
    for row in range(rows):
        place = rows * source + row
        same = lax.rem(place, half) == lax.rem(target, half)
        sign = jnp.where((target >= half) & (place >= half), -1.0, 1.0)
        mixes.append(jnp.where(same, sign, 0.0).astype(jnp.bfloat16))
    half_lanes = LANE // 2
    for slot in range(high):
        block = work[pl.ds(slot, parts, stride=high), :].T.astype(jnp.bfloat16)
        result = jnp.dot(block[:half_lanes], mixes[0], preferred_element_type=jnp.float32)
        result = result + jnp.dot(block[half_lanes:], mixes[1], preferred_element_type=jnp.float32)
        quarter = half_lanes // 2
        out_ref[slot] = result[:quarter].reshape(out_ref.shape[1:])
        if high + slot < slots:
            out_ref[high + slot] = result[quarter:].reshape(out_ref.shape[1:])


def shift_all(blocks, axis):
    count = lax.axis_size(axis)
    moved = [blocks[0]]
    for shift in range(1, count):
        moved.append(lax.ppermute(blocks[shift], axis, [(i, (i + shift) % count) for i in range(count)]))
    return moved


def body(adjoint_grid, lower_diffusion, upper_diffusion, row_lengths, wave_order):
    lev_count = lax.axis_size("lev")
    lat_count = lax.axis_size("lat")
    levels, rows, fields, points = adjoint_grid.shape
    waves = wave_order.shape[0]
    block, step, window = sizes(points, lev_count)
    f32, bf16 = jnp.float32, jnp.bfloat16
    members = levels * fields
    shape = jax.ShapeDtypeStruct
    packed = pl.pallas_call(
        lambda *refs: pack_kernel(lev_count, points, *refs),
        out_shape=[shape((rows, members, window), bf16)] * lev_count,
        in_specs=[VMEM],
        out_specs=[VMEM] * lev_count,
        name="pack",
    )(adjoint_grid)
    factor = shape((lev_count, rows, members, window), f32)
    fine, coarse, first, second, third = pl.pallas_call(
        lambda *refs: prepare_kernel(lev_count, points, *refs),
        out_shape=[shape((rows, DEEP, 2 * waves), bf16), shape((rows, 2, 24, waves), f32), factor, factor, factor],
        in_specs=[SMEM, VMEM, VMEM, VMEM],
        out_specs=[VMEM] * 5,
        name="prepare",
        cost_estimate=pl.CostEstimate(flops=20_000_000, bytes_accessed=4_000_000, transcendentals=0),
    )(row_lengths, wave_order[None, :], lower_diffusion, upper_diffusion)
    arrived = shift_all(packed, "lev")
    solved = pl.pallas_call(
        lambda *refs: solve_kernel(lev_count, points, *refs),
        out_shape=[shape((rows, members, window), bf16)] * lev_count,
        in_specs=[SMEM] + [VMEM] * (3 + lev_count),
        out_specs=[VMEM] * lev_count,
        scratch_shapes=[pltpu.VMEM((lev_count, rows, members, window), f32)],
        name="solve",
    )(row_lengths, first, second, third, *arrived)
    returned = shift_all(solved, "lev")
    slots = waves // lat_count
    high = 24
    sent = pl.pallas_call(
        lambda *refs: fourier_kernel(lev_count, points, *refs),
        out_shape=shape((lat_count, high, LANE), bf16),
        in_specs=[VMEM] * (2 + lev_count),
        out_specs=VMEM,
        scratch_shapes=[pltpu.VMEM((rows, 2, waves // LANE, members, LANE), f32), pltpu.VMEM((waves + 16, LANE), f32)],
        name="fourier",
    )(fine, coarse, *returned)
    received = lax.all_to_all(sent, "lat", split_axis=0, concat_axis=0, tiled=True)
    return pl.pallas_call(
        pair_kernel,
        out_shape=shape((slots, 2, fields, levels, rows * lat_count), f32),
        in_specs=[VMEM],
        out_specs=VMEM,
        scratch_shapes=[pltpu.VMEM((lat_count * high, LANE), f32)],
        name="pair",
    )(received)


def solution(mesh):
    in_specs = (P("lev", "lat", None, None), P(None, "lat", "lev"), P(None, "lat", "lev"), P(), P())
    out_specs = P("lat", None, None, "lev", None)
    return jax.shard_map(body, mesh=mesh, in_specs=in_specs, out_specs=out_specs, check_vma=False)
```

time: 908 us -> 52.7 us (0.06)
  other arithmetic: 748 us -> 0 us
  local copies, waits for them, and re-layouts: 90.8 us -> 2.61 us
  matrix products: 20.7 us -> 0 us
  Pallas kernels: 0 us -> 18.5 us
    convert_element_type x2 -> x0, other arithmetic: 722 us -> none  [fourier_basis(): cos_part = jnp.where(inside, jnp.cos(phase_angle), 0.0).astype(jnp.bfloat16)]
    unnamed x9 -> x12, local copies, waits for them, and re-layouts: 42.9 us -> 1.32 us
    dot_general x2 -> x0, matrix products: 20.7 us -> none  [one_row(): product = jnp.dot(flattened, basis, preferred_element_type=jnp.float32)]
    pallas_call x0 -> x5, Pallas kernels: none -> 18.5 us  [the longest x1 6.37 us: body(): pl.pallas_call(lambda *refs: prepare_kernel(lev_count, points, *refs), ou...]
    all_to_all x7 -> x0, local copies, waits for them, and re-layouts: 18.4 us -> none  [the longest x1 10.3 us: body(): lax.all_to_all(adjoint_grid, 'lev', split_axis=3, concat_axis=0, tiled=True)]
    gather x1 -> x0, local copies, waits for them, and re-layouts: 13.5 us -> none  [body(): ordered = jnp.take(spectra, wave_order, axis=4)]
    all_to_all x2 -> x0, starting transfers between devices: 9.61 us -> none  [the longest x1 5.98 us: body(): lax.all_to_all(adjoint_grid, 'lev', split_axis=3, concat_axis=0, tiled=True)]
  transfers between devices with their start and end apart: 3 -> 6, of which waited for: 2 -> 3; matrix products, arithmetic and copies ran while one was open for 1% -> 2% of each run, Pallas kernels for 0% -> 12%
where the time goes in v1:
time: 52.7 us; the launch traced here: 52.3 us
  Pallas kernels  18.5 us (35%)
  blocking collectives  18.1 us (34%)
  starting transfers between devices  9.68 us (18%)
  waiting for transfers between devices  3.44 us (7%)
  local copies, waits for them, and re-layouts  2.61 us (5%)
    all_to_all x1, blocking collectives, body(): lax.all_to_all(sent, 'lat', split_axis=0, concat_axis=0, tiled=True)  18.1 us
    ppermute x6, starting transfers between devices, shift_all(): lax.ppermute(blocks[shift], axis, [(i, (i + shift) % count) for i in rang...  9.68 us
    pallas_call x1, Pallas kernels, body(): pl.pallas_call(lambda *refs: prepare_kernel(lev_count, points, *refs), ou...  6.37 us
    pallas_call x1, Pallas kernels, body(): pl.pallas_call(lambda *refs: fourier_kernel(lev_count, points, *refs), ou...  4.45 us
    pallas_call x1, Pallas kernels, body(): pl.pallas_call(lambda *refs: solve_kernel(lev_count, points, *refs), out_...  3.46 us
    ppermute x6, waiting for transfers between devices, shift_all(): lax.ppermute(blocks[shift], axis, [(i, (i + shift) % count) for i in rang...  3.44 us
    pallas_call x1, Pallas kernels, body(): pl.pallas_call(pair_kernel, out_shape=shape((slots, 2, fields, levels, ro...  2.21 us
    pallas_call x1, Pallas kernels, body(): pl.pallas_call(lambda *refs: pack_kernel(lev_count, points, *refs), out_s...  1.99 us
  transfers between devices with their start and end apart: 6, of which 3 were waited for; matrix products, arithmetic and copies ran while one was open for 2% of the time, Pallas kernels for 12%

profile of v1, /device:TPU:1, one launch (start us, length us, event | category | flops | bytes accessed | tf_op | source)
XLA Modules:
  0.0 52.3 jit_solution(3462482670106525908)
XLA Ops:
  0.0 2.0 %pack.1 = (bf16[2,16,1408]{2,1,0:T(8,128)(2,1)}, bf16[2,16,1408]{2,1,0:T(8,128)(2,1)}, bf16[2,16,1408]{2,1,0:T(8,128)(2,1)}, bf16[2,16,1408]{2,1,0:T(8,128)(2,1)}) custom-call(bf16[8,2,2,5136]{3,2,1,0:T(2,128)(2,1)} %refs_0_.4), custom_call_target="tpu_custom_call" | custom-call | tf_op jit(solution)/shard_map/pack/pallas_call | solution.py:273
  2.0 2.5 %collective-permute-start = (bf16[2,16,1408]{2,1,0:T(8,128)(2,1)}, bf16[2,16,1408]{2,1,0:T(8,128)(2,1)S(1)}, u32[]{:S(2)}, u32[]{:S(2)}) collective-permute-start(bf16[2,16,1408]{2,1,0:T(8,128)(2,1)} %get-tuple-element.24), channel_id=1, source_target_pairs={{0,1},{1,2},{2,3},{3,0},{4,5},{5,6},{6,7},{7,4},{8,9},{9,10},{10,1... | collective-permute-start | bytes 270344 | tf_op jit(solution)/shard_map/ppermute | solution.py:260
  4.4 3.3 %collective-permute-start.1 = (bf16[2,16,1408]{2,1,0:T(8,128)(2,1)}, bf16[2,16,1408]{2,1,0:T(8,128)(2,1)S(1)}, u32[]{:S(2)}, u32[]{:S(2)}) collective-permute-start(bf16[2,16,1408]{2,1,0:T(8,128)(2,1)} %get-tuple-element.25), channel_id=1, source_target_pairs={{0,2},{1,3},{2,0},{3,1},{4,6},{5,7},{6,4},{7,5},{8,10},{9,11},{10,... | collective-permute-start | bytes 270344 | tf_op jit(solution)/shard_map/ppermute | solution.py:260
  7.8 0.7 %collective-permute-start.2 = (bf16[2,16,1408]{2,1,0:T(8,128)(2,1)}, bf16[2,16,1408]{2,1,0:T(8,128)(2,1)S(1)}, u32[]{:S(2)}, u32[]{:S(2)}) collective-permute-start(bf16[2,16,1408]{2,1,0:T(8,128)(2,1)} %get-tuple-element.26), channel_id=1, source_target_pairs={{0,3},{1,0},{2,1},{3,2},{4,7},{5,4},{6,5},{7,6},{8,11},{9,8},{10,9... | collective-permute-start | bytes 270344 | tf_op jit(solution)/shard_map/ppermute | solution.py:260
  8.5 1.3 %broadcast_in_dim.3.refs_1_ = s32[1,1280]{1,0:T(1,128)} reshape(s32[1280]{0:T(1024)} %param.9) | data formatting | bytes 10240 | tf_op jit(solution)/shard_map/broadcast_in_dim | solution.py:288
  9.8 6.4 %prepare.1 = (bf16[2,256,2560]{2,1,0:T(8,128)(2,1)}, f32[2,2,24,1280]{3,2,1,0:T(8,128)}, f32[4,2,16,1408]{3,2,1,0:T(8,128)}, f32[4,2,16,1408]{3,2,1,0:T(8,128)}, f32[4,2,16,1408]{3,2,1,0:T(8,128)}) custom-call(s32[32]{0:T(128)} %refs_0_.5, s32[1,1280]{1,0:T(1,128)} %broadcast_in_dim.3.refs_1_, f32[32,2,1284]{2,1,0:T(2,128)} %refs_2_.1, f32[32,2,1284]{2,1,0:T(2,128)} %refs_3_.1), custom_call_target="tpu_custom_call" | custom-call | flops 20000000 | bytes 4000000 | tf_op jit(solution)/shard_map/prepare/pallas_call | solution.py:281
  16.1 0.0 collective-permute-done.refs_5_
  16.1 0.0 copy-start
  16.1 0.0 collective-permute-done.1.refs_6_
  16.2 0.0 copy-start.1
  16.2 0.0 collective-permute-done.2.refs_7_
  16.2 0.0 copy-start.2
  16.2 0.6 %copy-done = bf16[2,16,1408]{2,1,0:T(8,128)(2,1)} copy-done((bf16[2,16,1408]{2,1,0:T(8,128)(2,1)}, bf16[2,16,1408]{2,1,0:T(8,128)(2,1)S(1)}, u32[]{:S(2)}) %copy-start) | copy-done | bytes 90136
  16.8 0.0 copy-done.1
  16.8 0.0 copy-done.2
  16.9 3.5 %solve.1 = (bf16[2,16,1408]{2,1,0:T(8,128)(2,1)}, bf16[2,16,1408]{2,1,0:T(8,128)(2,1)}, bf16[2,16,1408]{2,1,0:T(8,128)(2,1)}, bf16[2,16,1408]{2,1,0:T(8,128)(2,1)}) custom-call(s32[32]{0:T(128)} %refs_0_.5, f32[4,2,16,1408]{3,2,1,0:T(8,128)} %get-tuple-element.20.refs_1_, f32[4,2,16,1408]{3,2,1,0:T(8,128)} %get-tuple-element.21.refs_2_, ...), custom_call_target="tpu_custom_call" | custom-call | tf_op jit(solution)/shard_map/solve/pallas_call | solution.py:290
  20.3 0.7 %collective-permute-start.3 = (bf16[2,16,1408]{2,1,0:T(8,128)(2,1)}, bf16[2,16,1408]{2,1,0:T(8,128)(2,1)S(1)}, u32[]{:S(2)}, u32[]{:S(2)}) collective-permute-start(bf16[2,16,1408]{2,1,0:T(8,128)(2,1)} %get-tuple-element.28), channel_id=1, source_target_pairs={{0,1},{1,2},{2,3},{3,0},{4,5},{5,6},{6,7},{7,4},{8,9},{9,10},{10,1... | collective-permute-start | bytes 270344 | tf_op jit(solution)/shard_map/ppermute | solution.py:260
  21.1 0.4 collective-permute-start.4
  21.5 2.0 %collective-permute-start.5 = (bf16[2,16,1408]{2,1,0:T(8,128)(2,1)}, bf16[2,16,1408]{2,1,0:T(8,128)(2,1)S(1)}, u32[]{:S(2)}, u32[]{:S(2)}) collective-permute-start(bf16[2,16,1408]{2,1,0:T(8,128)(2,1)} %get-tuple-element.30), channel_id=1, source_target_pairs={{0,3},{1,0},{2,1},{3,2},{4,7},{5,4},{6,5},{7,6},{8,11},{9,8},{10,9... | collective-permute-start | bytes 270344 | tf_op jit(solution)/shard_map/ppermute | solution.py:260
  23.5 1.6 %collective-permute-done.3.refs_3_ = bf16[2,16,1408]{2,1,0:T(8,128)(2,1)S(1)} collective-permute-done((bf16[2,16,1408]{2,1,0:T(8,128)(2,1)}, bf16[2,16,1408]{2,1,0:T(8,128)(2,1)S(1)}, u32[]{:S(2)}, u32[]{:S(2)}) %collective-permute-start.3) | collective-permute-done | bytes 90144 | tf_op jit(solution)/shard_map/ppermute | solution.py:260
  25.1 0.0 copy-start.3
  25.1 1.2 %collective-permute-done.4.refs_4_ = bf16[2,16,1408]{2,1,0:T(8,128)(2,1)S(1)} collective-permute-done((bf16[2,16,1408]{2,1,0:T(8,128)(2,1)}, bf16[2,16,1408]{2,1,0:T(8,128)(2,1)S(1)}, u32[]{:S(2)}, u32[]{:S(2)}) %collective-permute-start.4) | collective-permute-done | bytes 90144 | tf_op jit(solution)/shard_map/ppermute | solution.py:260
  26.3 0.0 copy-start.4
  26.3 0.6 %collective-permute-done.5.refs_5_ = bf16[2,16,1408]{2,1,0:T(8,128)(2,1)S(1)} collective-permute-done((bf16[2,16,1408]{2,1,0:T(8,128)(2,1)}, bf16[2,16,1408]{2,1,0:T(8,128)(2,1)S(1)}, u32[]{:S(2)}, u32[]{:S(2)}) %collective-permute-start.5) | collective-permute-done | bytes 90144 | tf_op jit(solution)/shard_map/ppermute | solution.py:260
  27.0 0.0 copy-start.5
  27.0 0.0 copy-done.3
  27.0 0.0 copy-done.4
  27.0 0.6 %copy-done.5 = bf16[2,16,1408]{2,1,0:T(8,128)(2,1)} copy-done((bf16[2,16,1408]{2,1,0:T(8,128)(2,1)}, bf16[2,16,1408]{2,1,0:T(8,128)(2,1)S(1)}, u32[]{:S(2)}) %copy-start.5) | copy-done | bytes 90136
  27.6 4.4 %fourier.1 = bf16[32,24,128]{2,1,0:T(8,128)(2,1)} custom-call(bf16[2,256,2560]{2,1,0:T(8,128)(2,1)} %get-tuple-element.18.refs_0_, f32[2,2,24,1280]{3,2,1,0:T(8,128)} %get-tuple-element.19.refs_1_, bf16[2,16,1408]{2,1,0:T(8,128)(2,1)} %get-tuple-element.27.refs_2_, bf16[2,16,1408]{2,1,0:T(8,128)(2,1)} %copy-done.3, bf16[2,16,1408]{2,1,0:T(8,128)(2,1)} %copy-done.4, ...), custom_call_target="tpu_custom_call" | custom-call | tf_op jit(solution)/shard_map/fourier/pallas_call | solution.py:301
  32.1 18.1 %all_to_all.5.in_ref = bf16[32,24,128]{2,1,0:T(8,128)(2,1)} all-to-all(bf16[32,24,128]{2,1,0:T(8,128)(2,1)} %fourier.1), channel_id=1, replica_groups=mesh['lat'=32,'lev'=4] {'lat'}, dimensions={0} | all-to-all | bytes 393216 | tf_op jit(solution)/shard_map/all_to_all | solution.py:309
  50.1 2.2 %pair.1 = f32[40,2,2,8,64]{4,3,2,1,0:T(8,128)} custom-call(bf16[32,24,128]{2,1,0:T(8,128)(2,1)} %all_to_all.5.in_ref), custom_call_target="tpu_custom_call" | custom-call | tf_op jit(solution)/shard_map/pair/pallas_call | solution.py:310
Async XLA Ops:
  2.0 14.2 %collective-permute-start = (bf16[2,16,1408]{2,1,0:T(8,128)(2,1)}, bf16[2,16,1408]{2,1,0:T(8,128)(2,1)S(1)}, u32[]{:S(2)}, u32[]{:S(2)}) collective-permute-start(bf16[2,16,1408]{2,1,0:T(8,128)(2,1)} %get-tuple-element.24), channel_id=1, source_target_pairs={{0,1},{1,2},{2,3},{3,0},{4,5},{5,6},{6,7},{7,4},{8,9},{9,10},{10,1... | collective-permute-start | bytes 270344 | tf_op jit(solution)/shard_map/ppermute | solution.py:260
  4.4 11.7 %collective-permute-start.1 = (bf16[2,16,1408]{2,1,0:T(8,128)(2,1)}, bf16[2,16,1408]{2,1,0:T(8,128)(2,1)S(1)}, u32[]{:S(2)}, u32[]{:S(2)}) collective-permute-start(bf16[2,16,1408]{2,1,0:T(8,128)(2,1)} %get-tuple-element.25), channel_id=1, source_target_pairs={{0,2},{1,3},{2,0},{3,1},{4,6},{5,7},{6,4},{7,5},{8,10},{9,11},{10,... | collective-permute-start | bytes 270344 | tf_op jit(solution)/shard_map/ppermute | solution.py:260
  7.8 8.4 %collective-permute-start.2 = (bf16[2,16,1408]{2,1,0:T(8,128)(2,1)}, bf16[2,16,1408]{2,1,0:T(8,128)(2,1)S(1)}, u32[]{:S(2)}, u32[]{:S(2)}) collective-permute-start(bf16[2,16,1408]{2,1,0:T(8,128)(2,1)} %get-tuple-element.26), channel_id=1, source_target_pairs={{0,3},{1,0},{2,1},{3,2},{4,7},{5,4},{6,5},{7,6},{8,11},{9,8},{10,9... | collective-permute-start | bytes 270344 | tf_op jit(solution)/shard_map/ppermute | solution.py:260
  16.1 0.7 %copy-start = (bf16[2,16,1408]{2,1,0:T(8,128)(2,1)}, bf16[2,16,1408]{2,1,0:T(8,128)(2,1)S(1)}, u32[]{:S(2)}) copy-start(bf16[2,16,1408]{2,1,0:T(8,128)(2,1)S(1)} %collective-permute-done.refs_5_) | copy-start | bytes 270340
  16.2 0.7 %copy-start.1 = (bf16[2,16,1408]{2,1,0:T(8,128)(2,1)}, bf16[2,16,1408]{2,1,0:T(8,128)(2,1)S(1)}, u32[]{:S(2)}) copy-start(bf16[2,16,1408]{2,1,0:T(8,128)(2,1)S(1)} %collective-permute-done.1.refs_6_) | copy-start | bytes 270340
  16.2 0.7 %copy-start.2 = (bf16[2,16,1408]{2,1,0:T(8,128)(2,1)}, bf16[2,16,1408]{2,1,0:T(8,128)(2,1)S(1)}, u32[]{:S(2)}) copy-start(bf16[2,16,1408]{2,1,0:T(8,128)(2,1)S(1)} %collective-permute-done.2.refs_7_) | copy-start | bytes 270340
  20.3 4.8 %collective-permute-start.3 = (bf16[2,16,1408]{2,1,0:T(8,128)(2,1)}, bf16[2,16,1408]{2,1,0:T(8,128)(2,1)S(1)}, u32[]{:S(2)}, u32[]{:S(2)}) collective-permute-start(bf16[2,16,1408]{2,1,0:T(8,128)(2,1)} %get-tuple-element.28), channel_id=1, source_target_pairs={{0,1},{1,2},{2,3},{3,0},{4,5},{5,6},{6,7},{7,4},{8,9},{9,10},{10,1... | collective-permute-start | bytes 270344 | tf_op jit(solution)/shard_map/ppermute | solution.py:260
  21.1 5.2 %collective-permute-start.4 = (bf16[2,16,1408]{2,1,0:T(8,128)(2,1)}, bf16[2,16,1408]{2,1,0:T(8,128)(2,1)S(1)}, u32[]{:S(2)}, u32[]{:S(2)}) collective-permute-start(bf16[2,16,1408]{2,1,0:T(8,128)(2,1)} %get-tuple-element.29), channel_id=1, source_target_pairs={{0,2},{1,3},{2,0},{3,1},{4,6},{5,7},{6,4},{7,5},{8,10},{9,11},{10,... | collective-permute-start | bytes 270344 | tf_op jit(solution)/shard_map/ppermute | solution.py:260
  21.5 5.5 %collective-permute-start.5 = (bf16[2,16,1408]{2,1,0:T(8,128)(2,1)}, bf16[2,16,1408]{2,1,0:T(8,128)(2,1)S(1)}, u32[]{:S(2)}, u32[]{:S(2)}) collective-permute-start(bf16[2,16,1408]{2,1,0:T(8,128)(2,1)} %get-tuple-element.30), channel_id=1, source_target_pairs={{0,3},{1,0},{2,1},{3,2},{4,7},{5,4},{6,5},{7,6},{8,11},{9,8},{10,9... | collective-permute-start | bytes 270344 | tf_op jit(solution)/shard_map/ppermute | solution.py:260
  25.1 1.8 %copy-start.3 = (bf16[2,16,1408]{2,1,0:T(8,128)(2,1)}, bf16[2,16,1408]{2,1,0:T(8,128)(2,1)S(1)}, u32[]{:S(2)}) copy-start(bf16[2,16,1408]{2,1,0:T(8,128)(2,1)S(1)} %collective-permute-done.3.refs_3_) | copy-start | bytes 270340
  26.3 0.7 %copy-start.4 = (bf16[2,16,1408]{2,1,0:T(8,128)(2,1)}, bf16[2,16,1408]{2,1,0:T(8,128)(2,1)S(1)}, u32[]{:S(2)}) copy-start(bf16[2,16,1408]{2,1,0:T(8,128)(2,1)S(1)} %collective-permute-done.4.refs_4_) | copy-start | bytes 270340
  27.0 0.6 %copy-start.5 = (bf16[2,16,1408]{2,1,0:T(8,128)(2,1)}, bf16[2,16,1408]{2,1,0:T(8,128)(2,1)S(1)}, u32[]{:S(2)}) copy-start(bf16[2,16,1408]{2,1,0:T(8,128)(2,1)S(1)} %collective-permute-done.5.refs_5_) | copy-start | bytes 270340

commit v2 on v1

--- a/solution.py
+++ b/solution.py
@@ -7,9 +7,10 @@
 
 LANE = 128
 DEEP = 256
+LIMIT = pltpu.CompilerParams(vmem_limit_bytes=24 << 20)
 TWO_PI = 6.283185307179586
 VMEM = pl.BlockSpec(memory_space=pltpu.VMEM)
-SMEM = pl.BlockSpec(memory_space=pltpu.SMEM)
+ANY = pl.BlockSpec(memory_space=pl.ANY)
 
 
 def sizes(points, lev_count):
@@ -19,12 +20,22 @@
     return block, step, window
 
 
-def pack_kernel(lev_count, points, x_ref, *outs):
-    block, step, window = sizes(points, lev_count)
-    levels, rows, fields = x_ref.shape[:3]
+def pack_kernel(lev_count, shifts, x_hbm, lower_hbm, upper_hbm, lengths_hbm, *refs):
+    outs, (lower_ref, upper_ref, limit_ref, x_ref, lengths_ref, sems) = refs[: len(shifts)], refs[len(shifts) :]
+    levels, rows, fields, points = x_ref.shape
+    _, step, _ = sizes(points, lev_count)
     last = points - lev_count * step
     me = lax.axis_index("lev")
-    for shift, out in enumerate(outs):
+    copies = [
+        pltpu.make_async_copy(source, target, sems.at[i])
+        for i, (source, target) in enumerate(
+            [(x_hbm, x_ref), (lengths_hbm, lengths_ref), (lower_hbm, lower_ref), (upper_hbm, upper_ref)]
+        )
+    ]
+    for copy in copies:
+        copy.start()
+    copies[0].wait()
+    for shift, out in zip(shifts, outs):
         to = lax.rem(me + shift, lev_count)
         base = pl.multiple_of(to * step, LANE)
         for row in range(rows):
@@ -46,6 +57,14 @@
                 for level in range(levels):
                     low = fields * level
                     out[row, low : low + fields, step : step + last] = x_ref[level, row, :, lev_count * step :]
+
+    copies[1].wait()
+    first = rows * lax.axis_index("lat")
+    for row in range(rows):
+        whole = lengths_ref[lax.rem(first + row, lengths_ref.shape[0])]
+        limit_ref[row : row + 1, :] = jnp.full((1, LANE), whole, jnp.int32)
+    copies[2].wait()
+    copies[3].wait()
 
 
 def turn(multiple, length):
@@ -68,22 +87,15 @@
     return real, imag
 
 
-def prepare_kernel(
-    lev_count, points, lengths_ref, wave_ref, lower_ref, upper_ref, fine_ref, coarse_ref, first_ref, second_ref, third_ref
-):
-    block, step, window = sizes(points, lev_count)
+def table_kernel(limit_ref, wave_ref, after_ref, fine_ref, coarse_ref):
     rows = fine_ref.shape[0]
     waves = wave_ref.shape[1]
-    halves = lengths_ref.shape[0]
     wave = wave_ref[...].astype(jnp.float32)
-    me_lat = lax.axis_index("lat")
-    me_lev = lax.axis_index("lev")
     coarse_rows = coarse_ref.shape[2]
     small = lax.broadcasted_iota(jnp.int32, (16, 1), 0).astype(jnp.float32)
     blocks = lax.broadcasted_iota(jnp.int32, (coarse_rows, 1), 0).astype(jnp.float32)
     for row in range(rows):
-        whole = lengths_ref[lax.rem(me_lat * rows + row, halves)]
-        length = jnp.full((1, 1), whole, jnp.int32).astype(jnp.float32)
+        length = limit_ref[row : row + 1, :1].astype(jnp.float32)
         near_real, near_imag = turn(wave * small, length)
         far_real, far_imag = turn(wave * (16.0 * small), length)
         for part in range(16):
@@ -97,6 +109,11 @@
         coarse_ref[row, 0] = real * scale
         coarse_ref[row, 1] = imag * scale
 
+
+def factor_kernel(lev_count, points, lower_ref, upper_ref, after_ref, first_ref, second_ref, third_ref):
+    block, step, _ = sizes(points, lev_count)
+    rows = first_ref.shape[1]
+    me_lev = lax.axis_index("lev")
     levels = lower_ref.shape[0]
     own = first_ref.shape[2] // 2
     ratio = None
@@ -126,14 +143,12 @@
                 out[chunk, row] = pltpu.roll(out[chunk, row], me_lev * (block - step), 1)
 
 
-def solve_kernel(lev_count, points, lengths_ref, first_ref, second_ref, third_ref, *refs):
+def solve_kernel(lev_count, points, limit_ref, first_ref, second_ref, third_ref, *refs):
     block, step, window = sizes(points, lev_count)
     sources, outs, work = refs[:lev_count], refs[lev_count : 2 * lev_count], refs[-1]
     rows = work.shape[1]
     own = work.shape[2] // 2
     levels = lev_count * own
-    halves = lengths_ref.shape[0]
-    me_lat = lax.axis_index("lat")
     me_lev = lax.axis_index("lev")
     for shift, source in enumerate(sources):
         chunk = lax.rem(me_lev + lev_count - shift, lev_count)
@@ -143,7 +158,7 @@
     offset = me_lev * (block - step)
     inside = []
     for row in range(rows):
-        whole = lengths_ref[lax.rem(me_lat * rows + row, halves)]
+        whole = limit_ref[row : row + 1, :1]
         inside.append((lane >= offset) & (lane < offset + block) & (lane + me_lev * step < whole))
     for row in range(rows):
         part = None
@@ -166,7 +181,7 @@
 
 
 def fourier_kernel(lev_count, points, fine_ref, coarse_ref, *refs):
-    block, step, window = sizes(points, lev_count)
+    _, step, _ = sizes(points, lev_count)
     sources, out_ref, spectra, turned = refs[:lev_count], refs[-3], refs[-2], refs[-1]
     rows = fine_ref.shape[0]
     waves = fine_ref.shape[2] // 2
@@ -253,11 +268,19 @@
             out_ref[high + slot] = result[quarter:].reshape(out_ref.shape[1:])
 
 
-def shift_all(blocks, axis):
-    count = lax.axis_size(axis)
-    moved = [blocks[0]]
-    for shift in range(1, count):
-        moved.append(lax.ppermute(blocks[shift], axis, [(i, (i + shift) % count) for i in range(count)]))
+def near(x):
+    return pltpu.with_memory_space_constraint(x, pltpu.VMEM)
+
+
+def far(x):
+    return pltpu.with_memory_space_constraint(x, pltpu.HBM)
+
+
+def exchange(blocks, order):
+    count = lax.axis_size("lev")
+    moved = {0: blocks[0]}
+    for shift in order[:-1]:
+        moved[shift] = lax.ppermute(blocks[shift], "lev", [(i, (i + shift) % count) for i in range(count)])
     return moved
 
 
@@ -266,55 +289,82 @@
     lat_count = lax.axis_size("lat")
     levels, rows, fields, points = adjoint_grid.shape
     waves = wave_order.shape[0]
-    block, step, window = sizes(points, lev_count)
+    _, _, window = sizes(points, lev_count)
     f32, bf16 = jnp.float32, jnp.bfloat16
     members = levels * fields
-    shape = jax.ShapeDtypeStruct
-    packed = pl.pallas_call(
-        lambda *refs: pack_kernel(lev_count, points, *refs),
-        out_shape=[shape((rows, members, window), bf16)] * lev_count,
-        in_specs=[VMEM],
-        out_specs=[VMEM] * lev_count,
+    order = sorted(range(lev_count), key=lambda shift: -min(shift, lev_count - shift))
+    windows = pltpu.VMEM((rows, members, window), bf16)
+    made = pl.pallas_call(
+        lambda *refs: pack_kernel(lev_count, order, *refs),
+        out_shape=[windows] * lev_count
+        + [pltpu.VMEM(lower_diffusion.shape, f32)] * 2
+        + [pltpu.VMEM((rows, LANE), jnp.int32)],
+        in_specs=[ANY] * 4,
+        out_specs=[VMEM] * (lev_count + 3),
+        scratch_shapes=[
+            pltpu.VMEM(adjoint_grid.shape, bf16),
+            pltpu.SMEM(row_lengths.shape, jnp.int32),
+            pltpu.SemaphoreType.DMA((4,)),
+        ],
         name="pack",
-    )(adjoint_grid)
-    factor = shape((lev_count, rows, members, window), f32)
-    fine, coarse, first, second, third = pl.pallas_call(
-        lambda *refs: prepare_kernel(lev_count, points, *refs),
-        out_shape=[shape((rows, DEEP, 2 * waves), bf16), shape((rows, 2, 24, waves), f32), factor, factor, factor],
-        in_specs=[SMEM, VMEM, VMEM, VMEM],
-        out_specs=[VMEM] * 5,
-        name="prepare",
-        cost_estimate=pl.CostEstimate(flops=20_000_000, bytes_accessed=4_000_000, transcendentals=0),
-    )(row_lengths, wave_order[None, :], lower_diffusion, upper_diffusion)
-    arrived = shift_all(packed, "lev")
+        compiler_params=LIMIT,
+    )(*[far(x) for x in (adjoint_grid, lower_diffusion, upper_diffusion, row_lengths)])
+    packed = dict(zip(order, made))
+    lower, upper, limit = made[lev_count:]
+    arrived = exchange(packed, order)
+    factor = pltpu.VMEM((lev_count, rows, members, window), f32)
+    factors = pl.pallas_call(
+        lambda *refs: factor_kernel(lev_count, points, *refs),
+        out_shape=[factor] * 3,
+        in_specs=[VMEM, VMEM, ANY],
+        out_specs=[VMEM] * 3,
+        name="factor",
+        compiler_params=LIMIT,
+        cost_estimate=pl.CostEstimate(flops=10_000_000, bytes_accessed=4_000_000, transcendentals=0),
+    )(near(lower), near(upper), packed[0])
     solved = pl.pallas_call(
         lambda *refs: solve_kernel(lev_count, points, *refs),
-        out_shape=[shape((rows, members, window), bf16)] * lev_count,
-        in_specs=[SMEM] + [VMEM] * (3 + lev_count),
+        out_shape=[windows] * lev_count,
+        in_specs=[VMEM] * (4 + lev_count),
         out_specs=[VMEM] * lev_count,
         scratch_shapes=[pltpu.VMEM((lev_count, rows, members, window), f32)],
         name="solve",
-    )(row_lengths, first, second, third, *arrived)
-    returned = shift_all(solved, "lev")
+        compiler_params=LIMIT,
+    )(near(limit), *[near(x) for x in factors], *[near(arrived[shift]) for shift in range(lev_count)])
+    returned = exchange(solved, order)
+    fine, coarse = pl.pallas_call(
+        table_kernel,
+        out_shape=[pltpu.VMEM((rows, DEEP, 2 * waves), bf16), pltpu.VMEM((rows, 2, 24, waves), f32)],
+        in_specs=[VMEM, VMEM, ANY],
+        out_specs=[VMEM] * 2,
+        name="table",
+        compiler_params=LIMIT,
+        cost_estimate=pl.CostEstimate(flops=10_000_000, bytes_accessed=4_000_000, transcendentals=0),
+    )(near(limit), wave_order[None, :], solved[0])
     slots = waves // lat_count
     high = 24
     sent = pl.pallas_call(
         lambda *refs: fourier_kernel(lev_count, points, *refs),
-        out_shape=shape((lat_count, high, LANE), bf16),
+        out_shape=pltpu.VMEM((lat_count, high, LANE), bf16),
         in_specs=[VMEM] * (2 + lev_count),
         out_specs=VMEM,
-        scratch_shapes=[pltpu.VMEM((rows, 2, waves // LANE, members, LANE), f32), pltpu.VMEM((waves + 16, LANE), f32)],
+        scratch_shapes=[
+            pltpu.VMEM((rows, 2, waves // LANE, members, LANE), f32),
+            pltpu.VMEM((waves + 16, LANE), f32),
+        ],
         name="fourier",
-    )(fine, coarse, *returned)
+        compiler_params=LIMIT,
+    )(near(fine), near(coarse), *[near(returned[shift]) for shift in range(lev_count)])
     received = lax.all_to_all(sent, "lat", split_axis=0, concat_axis=0, tiled=True)
     return pl.pallas_call(
         pair_kernel,
-        out_shape=shape((slots, 2, fields, levels, rows * lat_count), f32),
+        out_shape=jax.ShapeDtypeStruct((slots, 2, fields, levels, rows * lat_count), f32),
         in_specs=[VMEM],
         out_specs=VMEM,
         scratch_shapes=[pltpu.VMEM((lat_count * high, LANE), f32)],
         name="pair",
-    )(received)
+        compiler_params=LIMIT,
+    )(near(received))
 
 
 def solution(mesh):

time: 52.7 us -> 40.8 us (0.77)
  Pallas kernels: 18.5 us -> 9.04 us
  local copies, waits for them, and re-layouts: 2.61 us -> 0.01 us
  starting transfers between devices: 9.68 us -> 11 us
  waiting for transfers between devices: 3.44 us -> 2.13 us
    pallas_call x3 -> x4, Pallas kernels: 10.6 us -> 6.03 us  [the longest x1 1.84 us: body(): pl.pallas_call(table_kernel, out_shape=[pltpu.VMEM((rows, DEEP, 2 * waves...]
    pallas_call x1, Pallas kernels: 4.45 us -> 1.82 us  [body(): pl.pallas_call(lambda *refs: fourier_kernel(lev_count, points, *refs), ou...]
    pallas_call x1, Pallas kernels: 3.46 us -> 1.19 us  [body(): pl.pallas_call(lambda *refs: solve_kernel(lev_count, points, *refs), out_...]
    ppermute x6, starting transfers between devices: 9.68 us -> 11 us  [exchange(): lax.ppermute(blocks[shift], 'lev', [(i, (i + shift) % count) for i in ran...]
    unnamed x12 -> x2, local copies, waits for them, and re-layouts: 1.32 us -> 0.01 us
    ppermute x6, waiting for transfers between devices: 3.44 us -> 2.13 us  [exchange(): lax.ppermute(blocks[shift], 'lev', [(i, (i + shift) % count) for i in ran...]
    broadcast_in_dim x1, local copies, waits for them, and re-layouts: 1.29 us -> 0.01 us  [body(): wave_order[None, :]]
  transfers between devices with their start and end apart: 6 -> 6, of which waited for: 3 -> 3; matrix products, arithmetic and copies ran while one was open for 2% -> 0% of each run, Pallas kernels for 12% -> 8%
where the time goes in v2:
time: 40.8 us; the launch traced here: 40.6 us
  blocking collectives  18.3 us (45%)
  starting transfers between devices  11 us (27%)
  Pallas kernels  9.04 us (22%)
  waiting for transfers between devices  2.13 us (5%)
    all_to_all x1, blocking collectives, body(): lax.all_to_all(sent, 'lat', split_axis=0, concat_axis=0, tiled=True)  18.3 us
    ppermute x6, starting transfers between devices, exchange(): lax.ppermute(blocks[shift], 'lev', [(i, (i + shift) % count) for i in ran...  11 us
    ppermute x6, waiting for transfers between devices, exchange(): lax.ppermute(blocks[shift], 'lev', [(i, (i + shift) % count) for i in ran...  2.13 us
    pallas_call x1, Pallas kernels, body(): pl.pallas_call(table_kernel, out_shape=[pltpu.VMEM((rows, DEEP, 2 * waves...  1.84 us
    pallas_call x1, Pallas kernels, body(): pl.pallas_call(lambda *refs: fourier_kernel(lev_count, points, *refs), ou...  1.82 us
    pallas_call x1, Pallas kernels, body(): pl.pallas_call(lambda *refs: factor_kernel(lev_count, points, *refs), out...  1.6 us
    pallas_call x1, Pallas kernels, body(): pl.pallas_call(lambda *refs: pack_kernel(lev_count, order, *refs), out_sh...  1.31 us
    pallas_call x1, Pallas kernels, body(): pl.pallas_call(pair_kernel, out_shape=jax.ShapeDtypeStruct((slots, 2, fie...  1.28 us
  transfers between devices with their start and end apart: 6, of which 3 were waited for; matrix products, arithmetic and copies ran while one was open for 0% of the time, Pallas kernels for 8%

profile of v2, /device:TPU:1, one launch (start us, length us, event | category | flops | bytes accessed | tf_op | source)
XLA Modules:
  0.0 40.6 jit_solution(11568099310382510544)
XLA Ops:
  0.0 0.0 copy-start
  0.0 1.3 %pack.1 = (bf16[2,16,1408]{2,1,0:T(8,128)(2,1)S(1)}, bf16[2,16,1408]{2,1,0:T(8,128)(2,1)S(1)}, bf16[2,16,1408]{2,1,0:T(8,128)(2,1)S(1)}, bf16[2,16,1408]{2,1,0:T...) custom-call(bf16[8,2,2,5136]{3,2,1,0:T(2,128)(2,1)} %refs_0_.1, ...), custom_call_target="tpu_custom_call" | custom-call | tf_op jit(solution)/shard_map/pack/pallas_call | solution.py:297
  1.3 2.5 %collective-permute-start = (bf16[2,16,1408]{2,1,0:T(8,128)(2,1)S(1)}, bf16[2,16,1408]{2,1,0:T(8,128)(2,1)S(1)}, u32[]{:S(2)}, u32[]{:S(2)}) collective-permute-start(bf16[2,16,1408]{2,1,0:T(8,128)(2,1)S(1)} %get-tuple-element.28), channel_id=1, source_target_pairs={{0,1},{1,2},{2,3},{3,0},{4,5},{5,6},{6,7},{7,4},{8,9},{9,10},{10,1... | collective-permute-start | bytes 270344 | tf_op jit(solution)/shard_map/ppermute | solution.py:283
  3.8 3.3 %collective-permute-start.1 = (bf16[2,16,1408]{2,1,0:T(8,128)(2,1)S(1)}, bf16[2,16,1408]{2,1,0:T(8,128)(2,1)S(1)}, u32[]{:S(2)}, u32[]{:S(2)}) collective-permute-start(bf16[2,16,1408]{2,1,0:T(8,128)(2,1)S(1)} %get-tuple-element.29), channel_id=1, source_target_pairs={{0,2},{1,3},{2,0},{3,1},{4,6},{5,7},{6,4},{7,5},{8,10},{9,11},{10,... | collective-permute-start | bytes 270344 | tf_op jit(solution)/shard_map/ppermute | solution.py:283
  7.1 0.7 %collective-permute-start.2 = (bf16[2,16,1408]{2,1,0:T(8,128)(2,1)S(1)}, bf16[2,16,1408]{2,1,0:T(8,128)(2,1)S(1)}, u32[]{:S(2)}, u32[]{:S(2)}) collective-permute-start(bf16[2,16,1408]{2,1,0:T(8,128)(2,1)S(1)} %get-tuple-element.30), channel_id=1, source_target_pairs={{0,3},{1,0},{2,1},{3,2},{4,7},{5,4},{6,5},{7,6},{8,11},{9,8},{10,9... | collective-permute-start | bytes 270344 | tf_op jit(solution)/shard_map/ppermute | solution.py:283
  7.9 1.6 %factor.1 = (f32[4,2,16,1408]{3,2,1,0:T(8,128)S(1)}, f32[4,2,16,1408]{3,2,1,0:T(8,128)S(1)}, f32[4,2,16,1408]{3,2,1,0:T(8,128)S(1)}) custom-call(f32[32,2,1284]{2,1,0:T(2,128)S(1)} %get-tuple-element.22.refs_0_, f32[32,2,1284]{2,1,0:T(2,128)S(1)} %get-tuple-element.23.refs_1_, bf16[2,16,1408]{2,1,0:T(8,128)(2,1)S(1)} %get-tuple-element.24.refs_2_.refs_4_), custom_call_target="tpu_custom_call" | custom-call | flops 10000000 | bytes 4000000 | tf_op jit(solution)/shard_map/factor/pallas_call | solution.py:316
  9.5 0.0 collective-permute-done.refs_5_
  9.5 1.3 %collective-permute-done.1.refs_6_ = bf16[2,16,1408]{2,1,0:T(8,128)(2,1)S(1)} collective-permute-done((bf16[2,16,1408]{2,1,0:T(8,128)(2,1)S(1)}, bf16[2,16,1408]{2,1,0:T(8,128)(2,1)S(1)}, u32[]{:S(2)}, u32[]{:S(2)}) %collective-permute-start.1) | collective-permute-done | bytes 90144 | tf_op jit(solution)/shard_map/ppermute | solution.py:283
  10.8 0.0 collective-permute-done.2.refs_7_
  10.8 1.2 %solve.1 = (bf16[2,16,1408]{2,1,0:T(8,128)(2,1)S(1)}, bf16[2,16,1408]{2,1,0:T(8,128)(2,1)S(1)}, bf16[2,16,1408]{2,1,0:T(8,128)(2,1)S(1)}, bf16[2,16,1408]{2,1,0:T(8,128)(2,1)S(1)}) custom-call(s32[2,128]{1,0:T(2,128)S(1)} %get-tuple-element.21.refs_0_.limit_ref, f32[4,2,16,1408]{3,2,1,0:T(8,128)S(1)} %get-tuple-element.25.refs_1_, ...), custom_call_target="tpu_custom_call" | custom-call | tf_op jit(solution)/shard_map/solve/pallas_call | solution.py:325
  12.0 2.0 %collective-permute-start.3 = (bf16[2,16,1408]{2,1,0:T(8,128)(2,1)S(1)}, bf16[2,16,1408]{2,1,0:T(8,128)(2,1)S(1)}, u32[]{:S(2)}, u32[]{:S(2)}) collective-permute-start(bf16[2,16,1408]{2,1,0:T(8,128)(2,1)S(1)} %get-tuple-element.34), channel_id=1, source_target_pairs={{0,1},{1,2},{2,3},{3,0},{4,5},{5,6},{6,7},{7,4},{8,9},{9,10},{10,1... | collective-permute-start | bytes 270344 | tf_op jit(solution)/shard_map/ppermute | solution.py:283
  14.0 1.5 %collective-permute-start.4 = (bf16[2,16,1408]{2,1,0:T(8,128)(2,1)S(1)}, bf16[2,16,1408]{2,1,0:T(8,128)(2,1)S(1)}, u32[]{:S(2)}, u32[]{:S(2)}) collective-permute-start(bf16[2,16,1408]{2,1,0:T(8,128)(2,1)S(1)} %get-tuple-element.35), channel_id=1, source_target_pairs={{0,2},{1,3},{2,0},{3,1},{4,6},{5,7},{6,4},{7,5},{8,10},{9,11},{10,... | collective-permute-start | bytes 270344 | tf_op jit(solution)/shard_map/ppermute | solution.py:283
  15.5 1.0 %collective-permute-start.5 = (bf16[2,16,1408]{2,1,0:T(8,128)(2,1)S(1)}, bf16[2,16,1408]{2,1,0:T(8,128)(2,1)S(1)}, u32[]{:S(2)}, u32[]{:S(2)}) collective-permute-start(bf16[2,16,1408]{2,1,0:T(8,128)(2,1)S(1)} %get-tuple-element.36), channel_id=1, source_target_pairs={{0,3},{1,0},{2,1},{3,2},{4,7},{5,4},{6,5},{7,6},{8,11},{9,8},{10,9... | collective-permute-start | bytes 270344 | tf_op jit(solution)/shard_map/ppermute | solution.py:283
  16.5 0.0 copy-done
  16.5 1.8 %table.1 = (bf16[2,256,2560]{2,1,0:T(8,128)(2,1)S(1)}, f32[2,2,24,1280]{3,2,1,0:T(8,128)S(1)}) custom-call(s32[2,128]{1,0:T(2,128)S(1)} %get-tuple-element.21.refs_0_.limit_ref, s32[1,1280]{1,0:T(1,128)S(1)} %broadcast_in_dim.3.wave_ref, bf16[2,16,1408]{2,1,0:T(8,128)(2,1)S(1)} %get-tuple-element.31.after_ref.refs_2_), custom_call_target="tpu_custom_call" | custom-call | flops 10000000 | bytes 4000000 | tf_op jit(solution)/shard_map/table/pallas_call | solution.py:335
  18.4 0.0 collective-permute-done.3.refs_3_
  18.4 0.7 %collective-permute-done.4.refs_4_ = bf16[2,16,1408]{2,1,0:T(8,128)(2,1)S(1)} collective-permute-done((bf16[2,16,1408]{2,1,0:T(8,128)(2,1)S(1)}, bf16[2,16,1408]{2,1,0:T(8,128)(2,1)S(1)}, u32[]{:S(2)}, u32[]{:S(2)}) %collective-permute-start.4) | collective-permute-done | bytes 90144 | tf_op jit(solution)/shard_map/ppermute | solution.py:283
  19.1 0.1 collective-permute-done.5.refs_5_
  19.2 1.8 %fourier.1 = bf16[32,24,128]{2,1,0:T(8,128)(2,1)S(1)} custom-call(bf16[2,256,2560]{2,1,0:T(8,128)(2,1)S(1)} %get-tuple-element.32.refs_0_, f32[2,2,24,1280]{3,2,1,0:T(8,128)S(1)} %get-tuple-element.33.refs_1_, bf16[2,16,1408]{2,1,0:T(8,128)(2,1)S(1)} %get-tuple-element.31.after_ref.refs_2_, bf16[2,16,1408]{2,1,0:T(8,128)(2,1)S(1)} %collective-permute-done.3.refs_3_, ...), custom_call_target="tpu_custom_call" | custom-call | tf_op jit(solution)/shard_map/fourier/pallas_call | solution.py:346
  21.0 18.3 %all_to_all.5.in_ref = bf16[32,24,128]{2,1,0:T(8,128)(2,1)S(1)} all-to-all(bf16[32,24,128]{2,1,0:T(8,128)(2,1)S(1)} %fourier.1), channel_id=1, replica_groups=mesh['lat'=32,'lev'=4] {'lat'}, dimensions={0} | all-to-all | bytes 393216 | tf_op jit(solution)/shard_map/all_to_all | solution.py:358
  39.3 1.3 %pair.1 = f32[40,2,2,8,64]{4,3,2,1,0:T(8,128)} custom-call(bf16[32,24,128]{2,1,0:T(8,128)(2,1)S(1)} %all_to_all.5.in_ref), custom_call_target="tpu_custom_call" | custom-call | tf_op jit(solution)/shard_map/pair/pallas_call | solution.py:359
  (1 shorter events, 0.0 us)
Async XLA Ops:
  0.0 16.5 %copy-start = (s32[1280]{0:T(1024)S(1)}, s32[1280]{0:T(1024)}, u32[]{:S(2)}) copy-start(s32[1280]{0:T(1024)} %param.9) | copy-start | bytes 15364
  1.3 8.2 %collective-permute-start = (bf16[2,16,1408]{2,1,0:T(8,128)(2,1)S(1)}, bf16[2,16,1408]{2,1,0:T(8,128)(2,1)S(1)}, u32[]{:S(2)}, u32[]{:S(2)}) collective-permute-start(bf16[2,16,1408]{2,1,0:T(8,128)(2,1)S(1)} %get-tuple-element.28), channel_id=1, source_target_pairs={{0,1},{1,2},{2,3},{3,0},{4,5},{5,6},{6,7},{7,4},{8,9},{9,10},{10,1... | collective-permute-start | bytes 270344 | tf_op jit(solution)/shard_map/ppermute | solution.py:283
  3.8 7.0 %collective-permute-start.1 = (bf16[2,16,1408]{2,1,0:T(8,128)(2,1)S(1)}, bf16[2,16,1408]{2,1,0:T(8,128)(2,1)S(1)}, u32[]{:S(2)}, u32[]{:S(2)}) collective-permute-start(bf16[2,16,1408]{2,1,0:T(8,128)(2,1)S(1)} %get-tuple-element.29), channel_id=1, source_target_pairs={{0,2},{1,3},{2,0},{3,1},{4,6},{5,7},{6,4},{7,5},{8,10},{9,11},{10,... | collective-permute-start | bytes 270344 | tf_op jit(solution)/shard_map/ppermute | solution.py:283
  7.1 3.7 %collective-permute-start.2 = (bf16[2,16,1408]{2,1,0:T(8,128)(2,1)S(1)}, bf16[2,16,1408]{2,1,0:T(8,128)(2,1)S(1)}, u32[]{:S(2)}, u32[]{:S(2)}) collective-permute-start(bf16[2,16,1408]{2,1,0:T(8,128)(2,1)S(1)} %get-tuple-element.30), channel_id=1, source_target_pairs={{0,3},{1,0},{2,1},{3,2},{4,7},{5,4},{6,5},{7,6},{8,11},{9,8},{10,9... | collective-permute-start | bytes 270344 | tf_op jit(solution)/shard_map/ppermute | solution.py:283
  12.0 6.3 %collective-permute-start.3 = (bf16[2,16,1408]{2,1,0:T(8,128)(2,1)S(1)}, bf16[2,16,1408]{2,1,0:T(8,128)(2,1)S(1)}, u32[]{:S(2)}, u32[]{:S(2)}) collective-permute-start(bf16[2,16,1408]{2,1,0:T(8,128)(2,1)S(1)} %get-tuple-element.34), channel_id=1, source_target_pairs={{0,1},{1,2},{2,3},{3,0},{4,5},{5,6},{6,7},{7,4},{8,9},{9,10},{10,1... | collective-permute-start | bytes 270344 | tf_op jit(solution)/shard_map/ppermute | solution.py:283
  14.0 5.1 %collective-permute-start.4 = (bf16[2,16,1408]{2,1,0:T(8,128)(2,1)S(1)}, bf16[2,16,1408]{2,1,0:T(8,128)(2,1)S(1)}, u32[]{:S(2)}, u32[]{:S(2)}) collective-permute-start(bf16[2,16,1408]{2,1,0:T(8,128)(2,1)S(1)} %get-tuple-element.35), channel_id=1, source_target_pairs={{0,2},{1,3},{2,0},{3,1},{4,6},{5,7},{6,4},{7,5},{8,10},{9,11},{10,... | collective-permute-start | bytes 270344 | tf_op jit(solution)/shard_map/ppermute | solution.py:283
  15.5 3.7 %collective-permute-start.5 = (bf16[2,16,1408]{2,1,0:T(8,128)(2,1)S(1)}, bf16[2,16,1408]{2,1,0:T(8,128)(2,1)S(1)}, u32[]{:S(2)}, u32[]{:S(2)}) collective-permute-start(bf16[2,16,1408]{2,1,0:T(8,128)(2,1)S(1)} %get-tuple-element.36), channel_id=1, source_target_pairs={{0,3},{1,0},{2,1},{3,2},{4,7},{5,4},{6,5},{7,6},{8,11},{9,8},{10,9... | collective-permute-start | bytes 270344 | tf_op jit(solution)/shard_map/ppermute | solution.py:283

commit v3 on v2

v3 whole, which is shorter than its diff:
```python
import jax
import jax.numpy as jnp
from jax import lax
from jax.experimental import pallas as pl
from jax.experimental.pallas import tpu as pltpu
from jax.sharding import PartitionSpec as P

LANE = 128
DEEP = 256
LIMIT = pltpu.CompilerParams(vmem_limit_bytes=24 << 20)
TWO_PI = 6.283185307179586
VMEM = pl.BlockSpec(memory_space=pltpu.VMEM)
ANY = pl.BlockSpec(memory_space=pl.ANY)


def sizes(points, lev_count):
    block = points // lev_count
    step = block // LANE * LANE
    window = step + LANE
    return block, step, window


def pack_kernel(lev_count, shifts, x_hbm, lengths_hbm, *refs):
    outs, (limit_ref, x_ref, lengths_ref, sems) = refs[: len(shifts)], refs[len(shifts) :]
    levels, rows, fields, points = x_ref.shape
    _, step, _ = sizes(points, lev_count)
    last = points - lev_count * step
    me = lax.axis_index("lev")
    pairs = [(x_hbm.at[level], x_ref.at[level]) for level in range(levels)]
    pairs += [(lengths_hbm, lengths_ref)]
    copies = [pltpu.make_async_copy(source, target, sems.at[i]) for i, (source, target) in enumerate(pairs)]
    for copy in copies:
        copy.start()
    pieces = len(copies) - 1
    for piece in range(pieces):
        copies[piece].wait()
        some = range(levels * piece // pieces, levels * (piece + 1) // pieces)
        for shift, out in zip(shifts, outs):
            to = lax.rem(me + shift, lev_count)
            base = pl.multiple_of(to * step, LANE)
            for level in some:
                for row in range(rows):
                    low = fields * (rows * level + row)
                    out[low : low + fields, :step] = x_ref[level, row, :, pl.ds(base, step)]
    for shift, out in zip(shifts, outs):
        to = lax.rem(me + shift, lev_count)

        @pl.when(to < lev_count - 1)
        def _():
            tail = pl.multiple_of(to * step + step, LANE)
            for level in range(levels):
                for row in range(rows):
                    low = fields * (rows * level + row)
                    out[low : low + fields, step:] = x_ref[level, row, :, pl.ds(tail, LANE)]

        @pl.when(to == lev_count - 1)
        def _():
            for level in range(levels):
                for row in range(rows):
                    low = fields * (rows * level + row)
                    out[low : low + fields, step : step + last] = x_ref[level, row, :, lev_count * step :]

    copies[-1].wait()
    first = rows * lax.axis_index("lat")
    for row in range(rows):
        whole = lengths_ref[lax.rem(first + row, lengths_ref.shape[0])]
        limit_ref[row : row + 1, :] = jnp.full((1, LANE), whole, jnp.int32)


def turn(multiple, length):
    inverse = 1.0 / length
    rest = multiple - jnp.floor(multiple * inverse) * length
    rest = jnp.where(rest < 0.0, rest + length, rest)
    rest = jnp.where(rest >= length, rest - length, rest)
    quarter = jnp.floor(4.0 * rest * inverse + 0.5)
    angle = (4.0 * rest - quarter * length) * ((TWO_PI / 4.0) * inverse)
    square = angle * angle
    sine = angle + angle * square * (-1.6666654611e-1 + square * (8.3321608736e-3 + square * -1.9515295891e-4))
    cosine = 1.0 - 0.5 * square + square * square * (
        4.166664568298827e-2 + square * (-1.388731625493765e-3 + square * 2.443315711809948e-5)
    )
    odd = (quarter == 1.0) | (quarter == 3.0)
    real = jnp.where(odd, sine, cosine)
    imag = jnp.where(odd, cosine, sine)
    real = jnp.where((quarter == 1.0) | (quarter == 2.0), -real, real)
    imag = jnp.where((quarter == 2.0) | (quarter == 3.0), imag, -imag)
    return real, imag


def table_kernel(limit_ref, wave_ref, after_ref, fine_ref, coarse_ref):
    rows = fine_ref.shape[0]
    waves = wave_ref.shape[1]
    wave = wave_ref[...].astype(jnp.float32)
    coarse_rows = coarse_ref.shape[2]
    small = lax.broadcasted_iota(jnp.int32, (16, 1), 0).astype(jnp.float32)
    blocks = lax.broadcasted_iota(jnp.int32, (coarse_rows, 1), 0).astype(jnp.float32)
    for row in range(rows):
        length = limit_ref[row : row + 1, :1].astype(jnp.float32)
        near_real, near_imag = turn(wave * small, length)
        far_real, far_imag = turn(wave * (16.0 * small), length)
        for part in range(16):
            one_real = far_real[part : part + 1]
            one_imag = far_imag[part : part + 1]
            low = 16 * part
            fine_ref[row, low : low + 16, :waves] = (near_real * one_real - near_imag * one_imag).astype(jnp.bfloat16)
            fine_ref[row, low : low + 16, waves:] = (near_real * one_imag + near_imag * one_real).astype(jnp.bfloat16)
        real, imag = turn(wave * (float(DEEP) * blocks), length)
        scale = jnp.where(2.0 * wave < length, 1.0 / jnp.sqrt(length), 0.0)
        coarse_ref[row, 0] = real * scale
        coarse_ref[row, 1] = imag * scale


def factor_kernel(
    lev_count, points, fields, lower_hbm, upper_hbm, after_ref, first_ref, second_ref, third_ref, lower_ref, upper_ref, sems
):
    block, step, _ = sizes(points, lev_count)
    levels, rows = lower_ref.shape[:2]
    copies = [
        pltpu.make_async_copy(lower_hbm, lower_ref, sems.at[0]),
        pltpu.make_async_copy(upper_hbm, upper_ref, sems.at[1]),
    ]
    for copy in copies:
        copy.start()
    for copy in copies:
        copy.wait()
    me_lev = lax.axis_index("lev")
    own = levels // lev_count
    ratio = None
    for level in range(levels):
        upper = upper_ref[level]
        if level == 0:
            pivot = 1.0 + upper
            above = jnp.zeros_like(upper)
        else:
            diagonal = 1.0 + lower_ref[level]
            if level < levels - 1:
                diagonal = diagonal + upper
            above = upper_ref[level - 1]
            pivot = diagonal + above * ratio
        inverse = 1.0 / pivot
        if level < levels - 1:
            ratio = -lower_ref[level + 1] * inverse
        else:
            ratio = jnp.zeros_like(inverse)
        chunk, inner = divmod(level, own)
        for out, value in ((first_ref, inverse), (second_ref, above * inverse), (third_ref, ratio)):
            for row in range(rows):
                low = fields * (rows * inner + row)
                out[chunk, low : low + fields, :block] = jnp.broadcast_to(value[row : row + 1], (fields, block))
    for out in (first_ref, second_ref, third_ref):
        for chunk in range(out.shape[0]):
            out[chunk] = pltpu.roll(out[chunk], me_lev * (block - step), 1)


def solve_kernel(lev_count, points, fields, limit_ref, first_ref, second_ref, third_ref, *refs):
    block, step, window = sizes(points, lev_count)
    sources, outs, work, done = refs[:lev_count], refs[lev_count : 2 * lev_count], refs[-2], refs[-1]
    rows, members = done.shape[1:3]
    own = members // fields
    levels = lev_count * own
    wide = rows * fields
    me_lev = lax.axis_index("lev")
    for shift, source in enumerate(sources):
        chunk = lax.rem(me_lev + lev_count - shift, lev_count)
        work[chunk] = source[...].astype(jnp.float32)
    lane = lax.broadcasted_iota(jnp.int32, (1, window), 1)
    offset = me_lev * (block - step)
    inside = []
    for row in range(rows):
        whole = limit_ref[row : row + 1, :1]
        inside.append((lane >= offset) & (lane < offset + block) & (lane + me_lev * step < whole))
    part = None
    for level in range(levels):
        chunk, inner = divmod(level, own)
        at = (chunk, slice(wide * inner, wide * (inner + 1)))
        value = work[at] * first_ref[at]
        part = value if part is None else value + second_ref[at] * part
        work[at] = part
    current = None
    for level in range(levels - 1, -1, -1):
        chunk, inner = divmod(level, own)
        at = (chunk, slice(wide * inner, wide * (inner + 1)))
        current = work[at] if current is None else work[at] - third_ref[at] * current
        for row in range(rows):
            done[chunk, row, fields * inner : fields * (inner + 1)] = current[fields * row : fields * (row + 1)]
    for shift, out in enumerate(outs):
        chunk = lax.rem(me_lev + shift, lev_count)
        for row in range(rows):
            out[row] = jnp.where(inside[row], done[chunk, row], 0.0).astype(jnp.bfloat16)


def fourier_kernel(lev_count, points, fine_ref, coarse_ref, *refs):
    _, step, _ = sizes(points, lev_count)
    sources, out_ref, spectra, turned = refs[:lev_count], refs[-3], refs[-2], refs[-1]
    rows = fine_ref.shape[0]
    waves = fine_ref.shape[2] // 2
    per = step // DEEP
    me_lev = lax.axis_index("lev")
    members = sources[0].shape[1]
    final = [lax.rem(me_lev + lev_count - shift, lev_count) == lev_count - 1 for shift in range(lev_count)]
    for row in range(rows):
        tails = [source[row, :, step:] for source in sources]
        none = jnp.zeros_like(tails[0])
        pieces = []
        for shift, source in enumerate(sources):
            before = (shift + 1) % lev_count
            pieces.append(source[row, :, :LANE] + jnp.where(final[before], none, tails[before]))
            pieces[-1] = jnp.concatenate([pieces[-1], source[row, :, LANE:DEEP]], axis=1)
            pieces += [source[row, :, DEEP * a : DEEP * (a + 1)] for a in range(1, per)]
        beyond = none
        for shift in range(lev_count):
            beyond = jnp.where(final[shift], tails[shift], beyond)
        pieces.append(jnp.concatenate([beyond, none], axis=1))
        main = jnp.concatenate(pieces, axis=0)
        for tile in range(waves // DEEP):
            low = DEEP * tile
            main_cos = jnp.dot(main, fine_ref[row, :, low : low + DEEP], preferred_element_type=jnp.float32)
            main_sin = jnp.dot(
                main, fine_ref[row, :, waves + low : waves + low + DEEP], preferred_element_type=jnp.float32
            )
            real = jnp.zeros((members, DEEP), jnp.float32)
            imag = jnp.zeros((members, DEEP), jnp.float32)
            for piece in range(lev_count * per + 1):
                shift, a = divmod(piece, per)
                at = per * lax.rem(me_lev + lev_count - shift, lev_count) + a if shift < lev_count else per * lev_count
                pos = members * piece
                y_cos, y_sin = main_cos[pos : pos + members], main_sin[pos : pos + members]
                c = coarse_ref[row, 0, pl.ds(at, 1), low : low + DEEP]
                s = coarse_ref[row, 1, pl.ds(at, 1), low : low + DEEP]
                real = real + (y_cos * c - y_sin * s)
                imag = imag + (y_sin * c + y_cos * s)
            for half in range(DEEP // LANE):
                at = tile * (DEEP // LANE) + half
                spectra[row, 0, at] = real[:, LANE * half : LANE * (half + 1)]
                spectra[row, 1, at] = imag[:, LANE * half : LANE * (half + 1)]
    for tile in range(waves // LANE):
        low = LANE * tile
        pieces = []
        for row in range(rows):
            one = [
                spectra[row, c, tile, pl.ds(field, members // 2, stride=2), :] for c in range(2) for field in range(2)
            ]
            pieces += one + one
        turned[low : low + LANE, :] = jnp.concatenate(pieces, axis=0).T
    turned[waves:, :] = jnp.zeros((turned.shape[0] - waves, LANE), jnp.float32)
    parts = out_ref.shape[0]
    high = out_ref.shape[1]
    slots = waves // parts
    lane = lax.broadcasted_iota(jnp.int32, (high, LANE), 1)
    left = lax.rem(lane, LANE // 2) < LANE // 4
    for part in range(parts):
        top = turned[slots * part : slots * part + high, :]
        low = turned[slots * part + high : slots * part + 2 * high, :]
        out_ref[part] = jnp.where(left, top, low).astype(jnp.bfloat16)


def pair_kernel(in_ref, out_ref, work, made, sems):
    parts, high = in_ref.shape[:2]
    slots = out_ref.shape[0]
    grid_rows = out_ref.shape[4]
    rows = grid_rows // parts
    for part in range(parts):
        work[high * part : high * (part + 1), :] = in_ref[part].astype(jnp.float32)
    source = lax.broadcasted_iota(jnp.int32, (parts, grid_rows), 0)
    target = lax.broadcasted_iota(jnp.int32, (parts, grid_rows), 1)
    half = grid_rows // 2
    mixes = []
    for row in range(rows):
        place = rows * source + row
        same = lax.rem(place, half) == lax.rem(target, half)
        sign = jnp.where((target >= half) & (place >= half), -1.0, 1.0)
        mixes.append(jnp.where(same, sign, 0.0).astype(jnp.bfloat16))
    half_lanes = LANE // 2
    quarter = half_lanes // 2
    group = 4
    copies = []
    for begin in range(0, high, group):
        turned = [
            work[pl.ds(slot, parts, stride=high), :].T.astype(jnp.bfloat16) for slot in range(begin, begin + group)
        ]
        above = jnp.concatenate([block[:half_lanes] for block in turned], axis=0)
        below = jnp.concatenate([block[half_lanes:] for block in turned], axis=0)
        result = jnp.dot(above, mixes[0], preferred_element_type=jnp.float32)
        result = result + jnp.dot(below, mixes[1], preferred_element_type=jnp.float32)
        for slot in range(group):
            both = result[half_lanes * slot : half_lanes * (slot + 1)]
            made[begin + slot] = both[:quarter].reshape(made.shape[1:])
            if high + begin + slot < slots:
                made[high + begin + slot] = both[quarter:].reshape(made.shape[1:])
        for first in (begin, high + begin):
            if first < slots:
                copy = pltpu.make_async_copy(
                    made.at[first : first + group], out_ref.at[first : first + group], sems.at[len(copies)]
                )
                copy.start()
                copies.append(copy)
    for copy in copies:
        copy.wait()


def near(x):
    return pltpu.with_memory_space_constraint(x, pltpu.VMEM)


def far(x):
    return pltpu.with_memory_space_constraint(x, pltpu.HBM)


def exchange(blocks, order):
    count = lax.axis_size("lev")
    moved = {0: blocks[0]}
    for shift in order:
        moved[shift] = lax.ppermute(blocks[shift], "lev", [(i, (i + shift) % count) for i in range(count)])
    return moved


def body(adjoint_grid, lower_diffusion, upper_diffusion, row_lengths, wave_order):
    lev_count = lax.axis_size("lev")
    lat_count = lax.axis_size("lat")
    levels, rows, fields, points = adjoint_grid.shape
    waves = wave_order.shape[0]
    _, _, window = sizes(points, lev_count)
    f32, bf16 = jnp.float32, jnp.bfloat16
    members = levels * fields
    order = sorted(range(lev_count), key=lambda shift: min(shift, lev_count - shift))
    farthest_first = sorted(order[1:], key=lambda shift: -min(shift, lev_count - shift))
    windows = pltpu.VMEM((rows, members, window), bf16)
    made = pl.pallas_call(
        lambda *refs: pack_kernel(lev_count, order, *refs),
        out_shape=[pltpu.VMEM((rows * members, window), bf16)] * lev_count
        + [pltpu.VMEM((rows, LANE), jnp.int32)],
        in_specs=[ANY] * 2,
        out_specs=[VMEM] * (lev_count + 1),
        scratch_shapes=[
            pltpu.VMEM(adjoint_grid.shape, bf16),
            pltpu.SMEM(row_lengths.shape, jnp.int32),
            pltpu.SemaphoreType.DMA((levels + 1,)),
        ],
        name="pack",
        compiler_params=LIMIT,
    )(far(adjoint_grid), far(row_lengths))
    packed = dict(zip(order, made))
    limit = made[-1]
    arrived = exchange(packed, order[1:])
    factor = pltpu.VMEM((lev_count, rows * members, window), f32)
    factors = pl.pallas_call(
        lambda *refs: factor_kernel(lev_count, points, fields, *refs),
        out_shape=[factor] * 3,
        in_specs=[ANY] * 3,
        out_specs=[VMEM] * 3,
        scratch_shapes=[
            pltpu.VMEM(lower_diffusion.shape, f32),
            pltpu.VMEM(upper_diffusion.shape, f32),
            pltpu.SemaphoreType.DMA((2,)),
        ],
        name="factor",
        compiler_params=LIMIT,
        cost_estimate=pl.CostEstimate(flops=10_000_000, bytes_accessed=4_000_000, transcendentals=0),
    )(far(lower_diffusion), far(upper_diffusion), packed[0])
    solved = pl.pallas_call(
        lambda *refs: solve_kernel(lev_count, points, fields, *refs),
        out_shape=[windows] * lev_count,
        in_specs=[VMEM] * (4 + lev_count),
        out_specs=[VMEM] * lev_count,
        scratch_shapes=[
            pltpu.VMEM((lev_count, rows * members, window), f32),
            pltpu.VMEM((lev_count, rows, members, window), f32),
        ],
        name="solve",
        compiler_params=LIMIT,
    )(near(limit), *[near(x) for x in factors], *[near(arrived[shift]) for shift in range(lev_count)])
    returned = exchange(solved, farthest_first)
    fine, coarse = pl.pallas_call(
        table_kernel,
        out_shape=[pltpu.VMEM((rows, DEEP, 2 * waves), bf16), pltpu.VMEM((rows, 2, 24, waves), f32)],
        in_specs=[VMEM, VMEM, ANY],
        out_specs=[VMEM] * 2,
        name="table",
        compiler_params=LIMIT,
        cost_estimate=pl.CostEstimate(flops=10_000_000, bytes_accessed=4_000_000, transcendentals=0),
    )(near(limit), wave_order[None, :], solved[0])
    slots = waves // lat_count
    high = 24
    sent = pl.pallas_call(
        lambda *refs: fourier_kernel(lev_count, points, *refs),
        out_shape=pltpu.VMEM((lat_count, high, LANE), bf16),
        in_specs=[VMEM] * (2 + lev_count),
        out_specs=VMEM,
        scratch_shapes=[
            pltpu.VMEM((rows, 2, waves // LANE, members, LANE), f32),
            pltpu.VMEM((waves + 16, LANE), f32),
        ],
        name="fourier",
        compiler_params=LIMIT,
    )(near(fine), near(coarse), *[near(returned[shift]) for shift in range(lev_count)])
    received = lax.all_to_all(sent, "lat", split_axis=0, concat_axis=0, tiled=True)
    return pl.pallas_call(
        pair_kernel,
        out_shape=jax.ShapeDtypeStruct((slots, 2, fields, levels, rows * lat_count), f32),
        in_specs=[VMEM],
        out_specs=ANY,
        scratch_shapes=[
            pltpu.VMEM((lat_count * high, LANE), f32),
            pltpu.VMEM((slots, 2, fields, levels, rows * lat_count), f32),
            pltpu.SemaphoreType.DMA((slots // 4,)),
        ],
        name="pair",
        compiler_params=LIMIT,
    )(near(received))


def solution(mesh):
    in_specs = (P("lev", "lat", None, None), P(None, "lat", "lev"), P(None, "lat", "lev"), P(), P())
    out_specs = P("lat", None, None, "lev", None)
    return jax.shard_map(body, mesh=mesh, in_specs=in_specs, out_specs=out_specs, check_vma=False)
```

time: 40.8 us -> 39.6 us (0.971)
  waiting for transfers between devices: 2.13 us -> 1 us
    ppermute x6, waiting for transfers between devices: 2.13 us -> 1 us  [exchange(): lax.ppermute(blocks[shift], 'lev', [(i, (i + shift) % count) for i in ran...]
    pallas_call x2, Pallas kernels: 2.79 us -> 3.47 us  [the longest x1 2.72 us: body(): pl.pallas_call(lambda *refs: factor_kernel(lev_count, points, fields, *re...]
    pallas_call x1, Pallas kernels: 1.82 us -> 1.24 us  [body(): pl.pallas_call(lambda *refs: fourier_kernel(lev_count, points, *refs), ou...]
  transfers between devices with their start and end apart: 6 -> 6, of which waited for: 3 -> 3; matrix products, arithmetic and copies ran while one was open for 0% -> 0% of each run, Pallas kernels for 8% -> 12%
where the time goes in v3:
time: 39.6 us; the launch traced here: 39.4 us
  blocking collectives  18.3 us (46%)
  starting transfers between devices  11 us (28%)
  Pallas kernels  8.92 us (23%)
  waiting for transfers between devices  1 us (3%)
    all_to_all x1, blocking collectives, body(): lax.all_to_all(sent, 'lat', split_axis=0, concat_axis=0, tiled=True)  18.3 us
    ppermute x6, starting transfers between devices, exchange(): lax.ppermute(blocks[shift], 'lev', [(i, (i + shift) % count) for i in ran...  11 us
    pallas_call x1, Pallas kernels, body(): pl.pallas_call(lambda *refs: factor_kernel(lev_count, points, fields, *re...  2.72 us
    pallas_call x1, Pallas kernels, body(): pl.pallas_call(table_kernel, out_shape=[pltpu.VMEM((rows, DEEP, 2 * waves...  1.84 us
    pallas_call x1, Pallas kernels, body(): pl.pallas_call(lambda *refs: fourier_kernel(lev_count, points, *refs), ou...  1.24 us
    pallas_call x1, Pallas kernels, body(): pl.pallas_call(pair_kernel, out_shape=jax.ShapeDtypeStruct((slots, 2, fie...  1.2 us
    pallas_call x1, Pallas kernels, body(): pl.pallas_call(lambda *refs: pack_kernel(lev_count, order, *refs), out_sh...  1.16 us
    ppermute x6, waiting for transfers between devices, exchange(): lax.ppermute(blocks[shift], 'lev', [(i, (i + shift) % count) for i in ran...  1 us
  transfers between devices with their start and end apart: 6, of which 3 were waited for; matrix products, arithmetic and copies ran while one was open for 0% of the time, Pallas kernels for 12%

profile of v3, /device:TPU:1, one launch (start us, length us, event | category | flops | bytes accessed | tf_op | source)
XLA Modules:
  0.0 39.4 jit_solution(11459172368331872332)
XLA Ops:
  0.0 0.0 copy-start
  0.0 1.2 %pack.1 = (bf16[32,1408]{1,0:T(8,128)(2,1)S(1)}, bf16[32,1408]{1,0:T(8,128)(2,1)S(1)}, bf16[32,1408]{1,0:T(8,128)(2,1)S(1)}, bf16[32,1408]{1,0:T(8,128)(2,1)S(1)}, s32[2,128]{1,0:T(2,128)S(1)}) custom-call(bf16[8,2,2,5136]{3,2,1,0:T(2,128)(2,1)} %refs_0_.2, s32[32]{0:T(128)} %refs_1_.2), custom_call_target="tpu_custom_call" | custom-call | tf_op jit(solution)/shard_map/pack/pallas_call | solution.py:328
  1.2 2.5 %collective-permute-start = (bf16[32,1408]{1,0:T(8,128)(2,1)S(1)}, bf16[32,1408]{1,0:T(8,128)(2,1)S(1)}, u32[]{:S(2)}, u32[]{:S(2)}) collective-permute-start(bf16[32,1408]{1,0:T(8,128)(2,1)S(1)} %get-tuple-element.24), channel_id=1, source_target_pairs={{0,1},{1,2},{2,3},{3,0},{4,5},{5,6},{6,7},{7,4},{8,9},{9,10},{10,1... | collective-permute-start | bytes 270344 | tf_op jit(solution)/shard_map/ppermute | solution.py:313
  3.7 3.3 %collective-permute-start.1 = (bf16[32,1408]{1,0:T(8,128)(2,1)S(1)}, bf16[32,1408]{1,0:T(8,128)(2,1)S(1)}, u32[]{:S(2)}, u32[]{:S(2)}) collective-permute-start(bf16[32,1408]{1,0:T(8,128)(2,1)S(1)} %get-tuple-element.25), channel_id=1, source_target_pairs={{0,2},{1,3},{2,0},{3,1},{4,6},{5,7},{6,4},{7,5},{8,10},{9,11},{10,... | collective-permute-start | bytes 270344 | tf_op jit(solution)/shard_map/ppermute | solution.py:313
  7.0 0.7 %collective-permute-start.2 = (bf16[32,1408]{1,0:T(8,128)(2,1)S(1)}, bf16[32,1408]{1,0:T(8,128)(2,1)S(1)}, u32[]{:S(2)}, u32[]{:S(2)}) collective-permute-start(bf16[32,1408]{1,0:T(8,128)(2,1)S(1)} %get-tuple-element.26), channel_id=1, source_target_pairs={{0,3},{1,0},{2,1},{3,2},{4,7},{5,4},{6,5},{7,6},{8,11},{9,8},{10,9... | collective-permute-start | bytes 270344 | tf_op jit(solution)/shard_map/ppermute | solution.py:313
  7.7 2.7 %factor.1 = (f32[4,32,1408]{2,1,0:T(8,128)S(1)}, f32[4,32,1408]{2,1,0:T(8,128)S(1)}, f32[4,32,1408]{2,1,0:T(8,128)S(1)}) custom-call(f32[32,2,1284]{2,1,0:T(2,128)} %refs_0_.3, f32[32,2,1284]{2,1,0:T(2,128)} %refs_1_.3, bf16[32,1408]{1,0:T(8,128)(2,1)S(1)} %get-tuple-element.20.refs_2_.refs_4_), custom_call_target="tpu_custom_call" | custom-call | flops 10000000 | bytes 4000000 | tf_op jit(solution)/shard_map/factor/pallas_call | solution.py:346
  10.5 0.0 collective-permute-done.refs_5_
  10.5 0.2 collective-permute-done.1.refs_6_
  10.7 0.0 collective-permute-done.2.refs_7_
  10.7 0.7 %solve.1 = (bf16[2,16,1408]{2,1,0:T(8,128)(2,1)S(1)}, bf16[2,16,1408]{2,1,0:T(8,128)(2,1)S(1)}, bf16[2,16,1408]{2,1,0:T(8,128)(2,1)S(1)}, bf16[2,16,1408]{2,1,0:T(8,128)(2,1)S(1)}) custom-call(s32[2,128]{1,0:T(2,128)S(1)} %get-tuple-element.19.refs_0_.limit_ref, f32[4,32,1408]{2,1,0:T(8,128)S(1)} %get-tuple-element.21.refs_1_, ...), custom_call_target="tpu_custom_call" | custom-call | tf_op jit(solution)/shard_map/solve/pallas_call | solution.py:360
  11.4 2.0 %collective-permute-start.3 = (bf16[2,16,1408]{2,1,0:T(8,128)(2,1)S(1)}, bf16[2,16,1408]{2,1,0:T(8,128)(2,1)S(1)}, u32[]{:S(2)}, u32[]{:S(2)}) collective-permute-start(bf16[2,16,1408]{2,1,0:T(8,128)(2,1)S(1)} %get-tuple-element.30), channel_id=1, source_target_pairs={{0,1},{1,2},{2,3},{3,0},{4,5},{5,6},{6,7},{7,4},{8,9},{9,10},{10,1... | collective-permute-start | bytes 270344 | tf_op jit(solution)/shard_map/ppermute | solution.py:313
  13.4 1.5 %collective-permute-start.4 = (bf16[2,16,1408]{2,1,0:T(8,128)(2,1)S(1)}, bf16[2,16,1408]{2,1,0:T(8,128)(2,1)S(1)}, u32[]{:S(2)}, u32[]{:S(2)}) collective-permute-start(bf16[2,16,1408]{2,1,0:T(8,128)(2,1)S(1)} %get-tuple-element.31), channel_id=1, source_target_pairs={{0,2},{1,3},{2,0},{3,1},{4,6},{5,7},{6,4},{7,5},{8,10},{9,11},{10,... | collective-permute-start | bytes 270344 | tf_op jit(solution)/shard_map/ppermute | solution.py:313
  14.9 1.0 %collective-permute-start.5 = (bf16[2,16,1408]{2,1,0:T(8,128)(2,1)S(1)}, bf16[2,16,1408]{2,1,0:T(8,128)(2,1)S(1)}, u32[]{:S(2)}, u32[]{:S(2)}) collective-permute-start(bf16[2,16,1408]{2,1,0:T(8,128)(2,1)S(1)} %get-tuple-element.32), channel_id=1, source_target_pairs={{0,3},{1,0},{2,1},{3,2},{4,7},{5,4},{6,5},{7,6},{8,11},{9,8},{10,9... | collective-permute-start | bytes 270344 | tf_op jit(solution)/shard_map/ppermute | solution.py:313
  15.9 0.0 copy-done
  15.9 1.8 %table.1 = (bf16[2,256,2560]{2,1,0:T(8,128)(2,1)S(1)}, f32[2,2,24,1280]{3,2,1,0:T(8,128)S(1)}) custom-call(s32[2,128]{1,0:T(2,128)S(1)} %get-tuple-element.19.refs_0_.limit_ref, s32[1,1280]{1,0:T(1,128)S(1)} %broadcast_in_dim.3.wave_ref, bf16[2,16,1408]{2,1,0:T(8,128)(2,1)S(1)} %get-tuple-element.27.after_ref.refs_2_), custom_call_target="tpu_custom_call" | custom-call | flops 10000000 | bytes 4000000 | tf_op jit(solution)/shard_map/table/pallas_call | solution.py:373
  17.8 0.0 collective-permute-done.3.refs_3_
  17.8 0.7 %collective-permute-done.4.refs_4_ = bf16[2,16,1408]{2,1,0:T(8,128)(2,1)S(1)} collective-permute-done((bf16[2,16,1408]{2,1,0:T(8,128)(2,1)S(1)}, bf16[2,16,1408]{2,1,0:T(8,128)(2,1)S(1)}, u32[]{:S(2)}, u32[]{:S(2)}) %collective-permute-start.4) | collective-permute-done | bytes 90144 | tf_op jit(solution)/shard_map/ppermute | solution.py:313
  18.5 0.1 collective-permute-done.5.refs_5_
  18.6 1.2 %fourier.1 = bf16[32,24,128]{2,1,0:T(8,128)(2,1)S(1)} custom-call(bf16[2,256,2560]{2,1,0:T(8,128)(2,1)S(1)} %get-tuple-element.28.refs_0_, f32[2,2,24,1280]{3,2,1,0:T(8,128)S(1)} %get-tuple-element.29.refs_1_, bf16[2,16,1408]{2,1,0:T(8,128)(2,1)S(1)} %get-tuple-element.27.after_ref.refs_2_, bf16[2,16,1408]{2,1,0:T(8,128)(2,1)S(1)} %collective-permute-done.3.refs_3_, ...), custom_call_target="tpu_custom_call" | custom-call | tf_op jit(solution)/shard_map/fourier/pallas_call | solution.py:384
  19.8 18.3 %all_to_all.5.in_ref = bf16[32,24,128]{2,1,0:T(8,128)(2,1)S(1)} all-to-all(bf16[32,24,128]{2,1,0:T(8,128)(2,1)S(1)} %fourier.1), channel_id=1, replica_groups=mesh['lat'=32,'lev'=4] {'lat'}, dimensions={0} | all-to-all | bytes 393216 | tf_op jit(solution)/shard_map/all_to_all | solution.py:396
  38.2 1.2 %pair.1 = f32[40,2,2,8,64]{4,3,2,1,0:T(8,128)} custom-call(bf16[32,24,128]{2,1,0:T(8,128)(2,1)S(1)} %all_to_all.5.in_ref), custom_call_target="tpu_custom_call" | custom-call | tf_op jit(solution)/shard_map/pair/pallas_call | solution.py:397
  (1 shorter events, 0.0 us)
Async XLA Ops:
  0.0 15.9 %copy-start = (s32[1280]{0:T(1024)S(1)}, s32[1280]{0:T(1024)}, u32[]{:S(2)}) copy-start(s32[1280]{0:T(1024)} %param.9) | copy-start | bytes 15364
  1.2 9.3 %collective-permute-start = (bf16[32,1408]{1,0:T(8,128)(2,1)S(1)}, bf16[32,1408]{1,0:T(8,128)(2,1)S(1)}, u32[]{:S(2)}, u32[]{:S(2)}) collective-permute-start(bf16[32,1408]{1,0:T(8,128)(2,1)S(1)} %get-tuple-element.24), channel_id=1, source_target_pairs={{0,1},{1,2},{2,3},{3,0},{4,5},{5,6},{6,7},{7,4},{8,9},{9,10},{10,1... | collective-permute-start | bytes 270344 | tf_op jit(solution)/shard_map/ppermute | solution.py:313
  3.7 7.0 %collective-permute-start.1 = (bf16[32,1408]{1,0:T(8,128)(2,1)S(1)}, bf16[32,1408]{1,0:T(8,128)(2,1)S(1)}, u32[]{:S(2)}, u32[]{:S(2)}) collective-permute-start(bf16[32,1408]{1,0:T(8,128)(2,1)S(1)} %get-tuple-element.25), channel_id=1, source_target_pairs={{0,2},{1,3},{2,0},{3,1},{4,6},{5,7},{6,4},{7,5},{8,10},{9,11},{10,... | collective-permute-start | bytes 270344 | tf_op jit(solution)/shard_map/ppermute | solution.py:313
  7.0 3.7 %collective-permute-start.2 = (bf16[32,1408]{1,0:T(8,128)(2,1)S(1)}, bf16[32,1408]{1,0:T(8,128)(2,1)S(1)}, u32[]{:S(2)}, u32[]{:S(2)}) collective-permute-start(bf16[32,1408]{1,0:T(8,128)(2,1)S(1)} %get-tuple-element.26), channel_id=1, source_target_pairs={{0,3},{1,0},{2,1},{3,2},{4,7},{5,4},{6,5},{7,6},{8,11},{9,8},{10,9... | collective-permute-start | bytes 270344 | tf_op jit(solution)/shard_map/ppermute | solution.py:313
  11.4 6.3 %collective-permute-start.3 = (bf16[2,16,1408]{2,1,0:T(8,128)(2,1)S(1)}, bf16[2,16,1408]{2,1,0:T(8,128)(2,1)S(1)}, u32[]{:S(2)}, u32[]{:S(2)}) collective-permute-start(bf16[2,16,1408]{2,1,0:T(8,128)(2,1)S(1)} %get-tuple-element.30), channel_id=1, source_target_pairs={{0,1},{1,2},{2,3},{3,0},{4,5},{5,6},{6,7},{7,4},{8,9},{9,10},{10,1... | collective-permute-start | bytes 270344 | tf_op jit(solution)/shard_map/ppermute | solution.py:313
  13.4 5.1 %collective-permute-start.4 = (bf16[2,16,1408]{2,1,0:T(8,128)(2,1)S(1)}, bf16[2,16,1408]{2,1,0:T(8,128)(2,1)S(1)}, u32[]{:S(2)}, u32[]{:S(2)}) collective-permute-start(bf16[2,16,1408]{2,1,0:T(8,128)(2,1)S(1)} %get-tuple-element.31), channel_id=1, source_target_pairs={{0,2},{1,3},{2,0},{3,1},{4,6},{5,7},{6,4},{7,5},{8,10},{9,11},{10,... | collective-permute-start | bytes 270344 | tf_op jit(solution)/shard_map/ppermute | solution.py:313
  14.9 3.7 %collective-permute-start.5 = (bf16[2,16,1408]{2,1,0:T(8,128)(2,1)S(1)}, bf16[2,16,1408]{2,1,0:T(8,128)(2,1)S(1)}, u32[]{:S(2)}, u32[]{:S(2)}) collective-permute-start(bf16[2,16,1408]{2,1,0:T(8,128)(2,1)S(1)} %get-tuple-element.32), channel_id=1, source_target_pairs={{0,3},{1,0},{2,1},{3,2},{4,7},{5,4},{6,5},{7,6},{8,11},{9,8},{10,9... | collective-permute-start | bytes 270344 | tf_op jit(solution)/shard_map/ppermute | solution.py:313

commit v4 on v3

--- a/solution.py
+++ b/solution.py
@@ -189,78 +189,110 @@
             out[row] = jnp.where(inside[row], done[chunk, row], 0.0).astype(jnp.bfloat16)
 
 
-def fourier_kernel(lev_count, points, fine_ref, coarse_ref, *refs):
+def blocks_sum(fine_ref, coarse_ref, row, tile, main, places, real, imag):
+    waves = fine_ref.shape[2] // 2
+    members = main.shape[0] // len(places)
+    low = DEEP * tile
+    all_cos = jnp.dot(main, fine_ref[row, :, low : low + DEEP], preferred_element_type=jnp.float32)
+    all_sin = jnp.dot(main, fine_ref[row, :, waves + low : waves + low + DEEP], preferred_element_type=jnp.float32)
+    for piece, place in enumerate(places):
+        pos = members * piece
+        y_cos, y_sin = all_cos[pos : pos + members], all_sin[pos : pos + members]
+        c = coarse_ref[row, 0, pl.ds(place, 1), low : low + DEEP]
+        s = coarse_ref[row, 1, pl.ds(place, 1), low : low + DEEP]
+        real = real + (y_cos * c - y_sin * s)
+        imag = imag + (y_sin * c + y_cos * s)
+    return real, imag
+
+
+def origin_of(shift, count):
+    return lax.rem(lax.axis_index("lev") + count - shift, count)
+
+
+def early_kernel(lev_count, points, shifts, fine_ref, coarse_ref, *refs):
     _, step, _ = sizes(points, lev_count)
+    sources, spectra = refs[:-1], refs[-1]
+    rows, _, _, members, _ = spectra.shape
+    waves = fine_ref.shape[2] // 2
+    per = step // DEEP
+    places = [per * origin_of(shift, lev_count) + a for shift in shifts for a in range(1, per)]
+    for row in range(rows):
+        main = jnp.concatenate(
+            [source[row, :, DEEP * a : DEEP * (a + 1)] for source in sources for a in range(1, per)], axis=0
+        )
+        for tile in range(waves // DEEP):
+            zero = jnp.zeros((members, DEEP), jnp.float32)
+            sums = blocks_sum(fine_ref, coarse_ref, row, tile, main, places, zero, zero)
+            for half in range(DEEP // LANE):
+                for part, value in enumerate(sums):
+                    spectra[row, part, tile * (DEEP // LANE) + half] = value[:, LANE * half : LANE * (half + 1)]
+
+
+def fourier_kernel(lev_count, points, early, fine_ref, coarse_ref, begun_ref, *refs):
+    block, step, _ = sizes(points, lev_count)
     sources, out_ref, spectra, turned = refs[:lev_count], refs[-3], refs[-2], refs[-1]
     rows = fine_ref.shape[0]
     waves = fine_ref.shape[2] // 2
     per = step // DEEP
-    me_lev = lax.axis_index("lev")
-    members = sources[0].shape[1]
-    final = [lax.rem(me_lev + lev_count - shift, lev_count) == lev_count - 1 for shift in range(lev_count)]
+    final = [origin_of(shift, lev_count) == lev_count - 1 for shift in range(lev_count)]
+    places = []
+    for shift in range(lev_count):
+        places += [per * origin_of(shift, lev_count) + a for a in range(1 if shift in early else per)]
+    places.append(per * lev_count)
     for row in range(rows):
         tails = [source[row, :, step:] for source in sources]
         none = jnp.zeros_like(tails[0])
         pieces = []
         for shift, source in enumerate(sources):
             before = (shift + 1) % lev_count
-            pieces.append(source[row, :, :LANE] + jnp.where(final[before], none, tails[before]))
-            pieces[-1] = jnp.concatenate([pieces[-1], source[row, :, LANE:DEEP]], axis=1)
-            pieces += [source[row, :, DEEP * a : DEEP * (a + 1)] for a in range(1, per)]
+            first = source[row, :, :LANE] + jnp.where(final[before], none, tails[before])
+            pieces.append(jnp.concatenate([first, source[row, :, LANE:DEEP]], axis=1))
+            if shift not in early:
+                pieces += [source[row, :, DEEP * a : DEEP * (a + 1)] for a in range(1, per)]
         beyond = none
         for shift in range(lev_count):
             beyond = jnp.where(final[shift], tails[shift], beyond)
         pieces.append(jnp.concatenate([beyond, none], axis=1))
         main = jnp.concatenate(pieces, axis=0)
         for tile in range(waves // DEEP):
-            low = DEEP * tile
-            main_cos = jnp.dot(main, fine_ref[row, :, low : low + DEEP], preferred_element_type=jnp.float32)
-            main_sin = jnp.dot(
-                main, fine_ref[row, :, waves + low : waves + low + DEEP], preferred_element_type=jnp.float32
-            )
-            real = jnp.zeros((members, DEEP), jnp.float32)
-            imag = jnp.zeros((members, DEEP), jnp.float32)
-            for piece in range(lev_count * per + 1):
-                shift, a = divmod(piece, per)
-                at = per * lax.rem(me_lev + lev_count - shift, lev_count) + a if shift < lev_count else per * lev_count
-                pos = members * piece
-                y_cos, y_sin = main_cos[pos : pos + members], main_sin[pos : pos + members]
-                c = coarse_ref[row, 0, pl.ds(at, 1), low : low + DEEP]
-                s = coarse_ref[row, 1, pl.ds(at, 1), low : low + DEEP]
-                real = real + (y_cos * c - y_sin * s)
-                imag = imag + (y_sin * c + y_cos * s)
-            for half in range(DEEP // LANE):
-                at = tile * (DEEP // LANE) + half
-                spectra[row, 0, at] = real[:, LANE * half : LANE * (half + 1)]
-                spectra[row, 1, at] = imag[:, LANE * half : LANE * (half + 1)]
+            halves = [tile * (DEEP // LANE) + half for half in range(DEEP // LANE)]
+            begun = [jnp.concatenate([begun_ref[row, part, at] for at in halves], axis=1) for part in range(2)]
+            sums = blocks_sum(fine_ref, coarse_ref, row, tile, main, places, *begun)
+            for half, at in enumerate(halves):
+                for part, value in enumerate(sums):
+                    spectra[row, part, at] = value[:, LANE * half : LANE * (half + 1)]
     for tile in range(waves // LANE):
         low = LANE * tile
         pieces = []
         for row in range(rows):
             one = [
-                spectra[row, c, tile, pl.ds(field, members // 2, stride=2), :] for c in range(2) for field in range(2)
+                spectra[row, c, tile, pl.ds(field, spectra.shape[3] // 2, stride=2), :] for c in range(2) for field in range(2)
             ]
             pieces += one + one
         turned[low : low + LANE, :] = jnp.concatenate(pieces, axis=0).T
-    turned[waves:, :] = jnp.zeros((turned.shape[0] - waves, LANE), jnp.float32)
-    parts = out_ref.shape[0]
-    high = out_ref.shape[1]
+    parts, groups, inner = out_ref.shape[:3]
+    high = groups * inner
     slots = waves // parts
     lane = lax.broadcasted_iota(jnp.int32, (high, LANE), 1)
     left = lax.rem(lane, LANE // 2) < LANE // 4
     for part in range(parts):
         top = turned[slots * part : slots * part + high, :]
-        low = turned[slots * part + high : slots * part + 2 * high, :]
-        out_ref[part] = jnp.where(left, top, low).astype(jnp.bfloat16)
+        low = turned[slots * part + high : slots * (part + 1), :]
+        block = jnp.where(left, top, low).astype(jnp.bfloat16)
+        for group in range(groups):
+            out_ref[part, group] = block[inner * group : inner * (group + 1)]
 
 
 def pair_kernel(in_ref, out_ref, work, made, sems):
-    parts, high = in_ref.shape[:2]
+    parts, groups, inner = in_ref.shape[:3]
+    high = groups * inner
     slots = out_ref.shape[0]
     grid_rows = out_ref.shape[4]
     rows = grid_rows // parts
     for part in range(parts):
-        work[high * part : high * (part + 1), :] = in_ref[part].astype(jnp.float32)
+        for group in range(groups):
+            low = high * part + inner * group
+            work[low : low + inner, :] = in_ref[part, group].astype(jnp.float32)
     source = lax.broadcasted_iota(jnp.int32, (parts, grid_rows), 0)
     target = lax.broadcasted_iota(jnp.int32, (parts, grid_rows), 1)
     half = grid_rows // 2
@@ -380,19 +412,28 @@
         cost_estimate=pl.CostEstimate(flops=10_000_000, bytes_accessed=4_000_000, transcendentals=0),
     )(near(limit), wave_order[None, :], solved[0])
     slots = waves // lat_count
-    high = 24
+    inner = 4
+    high = slots // 2
+    early = (0, farthest_first[0])
+    sums = pltpu.VMEM((rows, 2, waves // LANE, members, LANE), f32)
+    begun = pl.pallas_call(
+        lambda *refs: early_kernel(lev_count, points, early, *refs),
+        out_shape=sums,
+        in_specs=[VMEM] * (2 + len(early)),
+        out_specs=VMEM,
+        name="early",
+        cost_estimate=pl.CostEstimate(flops=500_000_000, bytes_accessed=4_000_000, transcendentals=0),
+        compiler_params=LIMIT,
+    )(near(fine), near(coarse), *[near(returned[shift]) for shift in early])
     sent = pl.pallas_call(
-        lambda *refs: fourier_kernel(lev_count, points, *refs),
-        out_shape=pltpu.VMEM((lat_count, high, LANE), bf16),
-        in_specs=[VMEM] * (2 + lev_count),
+        lambda *refs: fourier_kernel(lev_count, points, early, *refs),
+        out_shape=pltpu.VMEM((lat_count, high // inner, inner, LANE), bf16),
+        in_specs=[VMEM] * (3 + lev_count),
         out_specs=VMEM,
-        scratch_shapes=[
-            pltpu.VMEM((rows, 2, waves // LANE, members, LANE), f32),
-            pltpu.VMEM((waves + 16, LANE), f32),
-        ],
+        scratch_shapes=[sums, pltpu.VMEM((waves, LANE), f32)],
         name="fourier",
         compiler_params=LIMIT,
-    )(near(fine), near(coarse), *[near(returned[shift]) for shift in range(lev_count)])
+    )(near(fine), near(coarse), near(begun), *[near(returned[shift]) for shift in range(lev_count)])
     received = lax.all_to_all(sent, "lat", split_axis=0, concat_axis=0, tiled=True)
     return pl.pallas_call(
         pair_kernel,

time: 39.6 us -> 38.7 us (0.977)
  waiting for transfers between devices: 1 us -> 0.21 us
  blocking collectives: 18.3 us -> 17.9 us
    ppermute x6, waiting for transfers between devices: 1 us -> 0.21 us  [exchange(): lax.ppermute(blocks[shift], 'lev', [(i, (i + shift) % count) for i in ran...]
    all_to_all x1, blocking collectives: 18.3 us -> 17.9 us  [body(): lax.all_to_all(sent, 'lat', split_axis=0, concat_axis=0, tiled=True)]
    pallas_call x1 -> x2, Pallas kernels: 1.24 us -> 1.55 us  [the longest x1 0.97 us: body(): pl.pallas_call(lambda *refs: fourier_kernel(lev_count, points, early, *re...]
  transfers between devices with their start and end apart: 6 -> 6, of which waited for: 3 -> 1; matrix products, arithmetic and copies ran while one was open for 0% -> 0% of each run, Pallas kernels for 12% -> 13%
where the time goes in v4:
time: 38.7 us; the launch traced here: 38.4 us
  blocking collectives  17.9 us (46%)
  starting transfers between devices  11 us (28%)
  Pallas kernels  9.26 us (24%)
    all_to_all x1, blocking collectives, body(): lax.all_to_all(sent, 'lat', split_axis=0, concat_axis=0, tiled=True)  17.9 us
    ppermute x6, starting transfers between devices, exchange(): lax.ppermute(blocks[shift], 'lev', [(i, (i + shift) % count) for i in ran...  11 us
    pallas_call x1, Pallas kernels, body(): pl.pallas_call(lambda *refs: factor_kernel(lev_count, points, fields, *re...  2.72 us
    pallas_call x1, Pallas kernels, body(): pl.pallas_call(table_kernel, out_shape=[pltpu.VMEM((rows, DEEP, 2 * waves...  1.84 us
    pallas_call x1, Pallas kernels, body(): pl.pallas_call(pair_kernel, out_shape=jax.ShapeDtypeStruct((slots, 2, fie...  1.24 us
    pallas_call x1, Pallas kernels, body(): pl.pallas_call(lambda *refs: pack_kernel(lev_count, order, *refs), out_sh...  1.16 us
    pallas_call x1, Pallas kernels, body(): pl.pallas_call(lambda *refs: fourier_kernel(lev_count, points, early, *re...  0.97 us
  transfers between devices with their start and end apart: 6, of which 1 were waited for; matrix products, arithmetic and copies ran while one was open for 0% of the time, Pallas kernels for 13%

profile of v4, /device:TPU:1, one launch (start us, length us, event | category | flops | bytes accessed | tf_op | source)
XLA Modules:
  0.0 38.4 jit_solution(3902918850657408923)
XLA Ops:
  0.0 0.0 copy-start
  0.0 1.2 %pack.1 = (bf16[32,1408]{1,0:T(8,128)(2,1)S(1)}, bf16[32,1408]{1,0:T(8,128)(2,1)S(1)}, bf16[32,1408]{1,0:T(8,128)(2,1)S(1)}, bf16[32,1408]{1,0:T(8,128)(2,1)S(1)}, s32[2,128]{1,0:T(2,128)S(1)}) custom-call(bf16[8,2,2,5136]{3,2,1,0:T(2,128)(2,1)} %refs_0_.2, s32[32]{0:T(128)} %refs_1_.2), custom_call_target="tpu_custom_call" | custom-call | tf_op jit(solution)/shard_map/pack/pallas_call | solution.py:360
  1.2 2.5 %collective-permute-start = (bf16[32,1408]{1,0:T(8,128)(2,1)S(1)}, bf16[32,1408]{1,0:T(8,128)(2,1)S(1)}, u32[]{:S(2)}, u32[]{:S(2)}) collective-permute-start(bf16[32,1408]{1,0:T(8,128)(2,1)S(1)} %get-tuple-element.24), channel_id=1, source_target_pairs={{0,1},{1,2},{2,3},{3,0},{4,5},{5,6},{6,7},{7,4},{8,9},{9,10},{10,1... | collective-permute-start | bytes 270344 | tf_op jit(solution)/shard_map/ppermute | solution.py:345
  3.7 3.3 %collective-permute-start.1 = (bf16[32,1408]{1,0:T(8,128)(2,1)S(1)}, bf16[32,1408]{1,0:T(8,128)(2,1)S(1)}, u32[]{:S(2)}, u32[]{:S(2)}) collective-permute-start(bf16[32,1408]{1,0:T(8,128)(2,1)S(1)} %get-tuple-element.25), channel_id=1, source_target_pairs={{0,2},{1,3},{2,0},{3,1},{4,6},{5,7},{6,4},{7,5},{8,10},{9,11},{10,... | collective-permute-start | bytes 270344 | tf_op jit(solution)/shard_map/ppermute | solution.py:345
  7.0 0.7 %collective-permute-start.2 = (bf16[32,1408]{1,0:T(8,128)(2,1)S(1)}, bf16[32,1408]{1,0:T(8,128)(2,1)S(1)}, u32[]{:S(2)}, u32[]{:S(2)}) collective-permute-start(bf16[32,1408]{1,0:T(8,128)(2,1)S(1)} %get-tuple-element.26), channel_id=1, source_target_pairs={{0,3},{1,0},{2,1},{3,2},{4,7},{5,4},{6,5},{7,6},{8,11},{9,8},{10,9... | collective-permute-start | bytes 270344 | tf_op jit(solution)/shard_map/ppermute | solution.py:345
  7.7 2.7 %factor.1 = (f32[4,32,1408]{2,1,0:T(8,128)S(1)}, f32[4,32,1408]{2,1,0:T(8,128)S(1)}, f32[4,32,1408]{2,1,0:T(8,128)S(1)}) custom-call(f32[32,2,1284]{2,1,0:T(2,128)} %refs_0_.3, f32[32,2,1284]{2,1,0:T(2,128)} %refs_1_.3, bf16[32,1408]{1,0:T(8,128)(2,1)S(1)} %get-tuple-element.20.refs_2_.refs_4_), custom_call_target="tpu_custom_call" | custom-call | flops 10000000 | bytes 4000000 | tf_op jit(solution)/shard_map/factor/pallas_call | solution.py:378
  10.5 0.0 collective-permute-done.refs_5_
  10.5 0.2 collective-permute-done.1.refs_6_
  10.7 0.0 collective-permute-done.2.refs_7_
  10.7 0.7 %solve.1 = (bf16[2,16,1408]{2,1,0:T(8,128)(2,1)S(1)}, bf16[2,16,1408]{2,1,0:T(8,128)(2,1)S(1)}, bf16[2,16,1408]{2,1,0:T(8,128)(2,1)S(1)}, bf16[2,16,1408]{2,1,0:T(8,128)(2,1)S(1)}) custom-call(s32[2,128]{1,0:T(2,128)S(1)} %get-tuple-element.19.refs_0_.limit_ref, f32[4,32,1408]{2,1,0:T(8,128)S(1)} %get-tuple-element.21.refs_1_, ...), custom_call_target="tpu_custom_call" | custom-call | tf_op jit(solution)/shard_map/solve/pallas_call | solution.py:392
  11.4 1.7 %collective-permute-start.3 = (bf16[2,16,1408]{2,1,0:T(8,128)(2,1)S(1)}, bf16[2,16,1408]{2,1,0:T(8,128)(2,1)S(1)}, u32[]{:S(2)}, u32[]{:S(2)}) collective-permute-start(bf16[2,16,1408]{2,1,0:T(8,128)(2,1)S(1)} %get-tuple-element.30), channel_id=1, source_target_pairs={{0,2},{1,3},{2,0},{3,1},{4,6},{5,7},{6,4},{7,5},{8,10},{9,11},{10,... | collective-permute-start | bytes 270344 | tf_op jit(solution)/shard_map/ppermute | solution.py:345
  13.1 1.2 %collective-permute-start.4 = (bf16[2,16,1408]{2,1,0:T(8,128)(2,1)S(1)}, bf16[2,16,1408]{2,1,0:T(8,128)(2,1)S(1)}, u32[]{:S(2)}, u32[]{:S(2)}) collective-permute-start(bf16[2,16,1408]{2,1,0:T(8,128)(2,1)S(1)} %get-tuple-element.31), channel_id=1, source_target_pairs={{0,1},{1,2},{2,3},{3,0},{4,5},{5,6},{6,7},{7,4},{8,9},{9,10},{10,1... | collective-permute-start | bytes 270344 | tf_op jit(solution)/shard_map/ppermute | solution.py:345
  14.3 1.5 %collective-permute-start.5 = (bf16[2,16,1408]{2,1,0:T(8,128)(2,1)S(1)}, bf16[2,16,1408]{2,1,0:T(8,128)(2,1)S(1)}, u32[]{:S(2)}, u32[]{:S(2)}) collective-permute-start(bf16[2,16,1408]{2,1,0:T(8,128)(2,1)S(1)} %get-tuple-element.32), channel_id=1, source_target_pairs={{0,3},{1,0},{2,1},{3,2},{4,7},{5,4},{6,5},{7,6},{8,11},{9,8},{10,9... | collective-permute-start | bytes 270344 | tf_op jit(solution)/shard_map/ppermute | solution.py:345
  15.8 0.0 copy-done
  15.8 1.8 %table.1 = (bf16[2,256,2560]{2,1,0:T(8,128)(2,1)S(1)}, f32[2,2,24,1280]{3,2,1,0:T(8,128)S(1)}) custom-call(s32[2,128]{1,0:T(2,128)S(1)} %get-tuple-element.19.refs_0_.limit_ref, s32[1,1280]{1,0:T(1,128)S(1)} %broadcast_in_dim.3.wave_ref, bf16[2,16,1408]{2,1,0:T(8,128)(2,1)S(1)} %get-tuple-element.27.after_ref.refs_2_.refs_3_), custom_call_target="tpu_custom_call" | custom-call | flops 10000000 | bytes 4000000 | tf_op jit(solution)/shard_map/table/pallas_call | solution.py:405
  17.7 0.0 collective-permute-done.3.refs_3_.refs_5_
  17.7 0.6 %early.1.refs_2_ = f32[2,2,10,16,128]{4,3,2,1,0:T(8,128)S(1)} custom-call(bf16[2,256,2560]{2,1,0:T(8,128)(2,1)S(1)} %get-tuple-element.28.refs_0_, f32[2,2,24,1280]{3,2,1,0:T(8,128)S(1)} %get-tuple-element.29.refs_1_, bf16[2,16,1408]{2,1,0:T(8,128)(2,1)S(1)} %get-tuple-element.27.after_ref.refs_2_.refs_3_, ...), custom_call_target="tpu_custom_call" | custom-call | flops 500000000 | bytes 4000000 | tf_op jit(solution)/shard_map/early/pallas_call | solution.py:419
  18.3 0.0 collective-permute-done.4.refs_4_
  18.3 0.0 collective-permute-done.5.refs_6_
  18.3 1.0 %fourier.1 = bf16[32,5,4,128]{3,2,1,0:T(4,128)(2,1)S(1)} custom-call(bf16[2,256,2560]{2,1,0:T(8,128)(2,1)S(1)} %get-tuple-element.28.refs_0_, f32[2,2,24,1280]{3,2,1,0:T(8,128)S(1)} %get-tuple-element.29.refs_1_, f32[2,2,10,16,128]{4,3,2,1,0:T(8,128)S(1)} %early.1.refs_2_, bf16[2,16,1408]{2,1,0:T(8,128)(2,1)S(1)} %get-tuple-element.27.after_ref.refs_2_.refs_3_, ...), custom_call_target="tpu_custom_call" | custom-call | tf_op jit(solution)/shard_map/fourier/pallas_call | solution.py:428
  19.3 17.9 %all_to_all.5.in_ref = bf16[32,5,4,128]{3,2,1,0:T(4,128)(2,1)S(1)} all-to-all(bf16[32,5,4,128]{3,2,1,0:T(4,128)(2,1)S(1)} %fourier.1), channel_id=1, replica_groups=mesh['lat'=32,'lev'=4] {'lat'}, dimensions={0} | all-to-all | bytes 327680 | tf_op jit(solution)/shard_map/all_to_all | solution.py:437
  37.2 1.2 %pair.1 = f32[40,2,2,8,64]{4,3,2,1,0:T(8,128)} custom-call(bf16[32,5,4,128]{3,2,1,0:T(4,128)(2,1)S(1)} %all_to_all.5.in_ref), custom_call_target="tpu_custom_call" | custom-call | tf_op jit(solution)/shard_map/pair/pallas_call | solution.py:438
  (1 shorter events, 0.0 us)
Async XLA Ops:
  0.0 15.8 %copy-start = (s32[1280]{0:T(1024)S(1)}, s32[1280]{0:T(1024)}, u32[]{:S(2)}) copy-start(s32[1280]{0:T(1024)} %param.9) | copy-start | bytes 15364
  1.2 9.3 %collective-permute-start = (bf16[32,1408]{1,0:T(8,128)(2,1)S(1)}, bf16[32,1408]{1,0:T(8,128)(2,1)S(1)}, u32[]{:S(2)}, u32[]{:S(2)}) collective-permute-start(bf16[32,1408]{1,0:T(8,128)(2,1)S(1)} %get-tuple-element.24), channel_id=1, source_target_pairs={{0,1},{1,2},{2,3},{3,0},{4,5},{5,6},{6,7},{7,4},{8,9},{9,10},{10,1... | collective-permute-start | bytes 270344 | tf_op jit(solution)/shard_map/ppermute | solution.py:345
  3.7 7.0 %collective-permute-start.1 = (bf16[32,1408]{1,0:T(8,128)(2,1)S(1)}, bf16[32,1408]{1,0:T(8,128)(2,1)S(1)}, u32[]{:S(2)}, u32[]{:S(2)}) collective-permute-start(bf16[32,1408]{1,0:T(8,128)(2,1)S(1)} %get-tuple-element.25), channel_id=1, source_target_pairs={{0,2},{1,3},{2,0},{3,1},{4,6},{5,7},{6,4},{7,5},{8,10},{9,11},{10,... | collective-permute-start | bytes 270344 | tf_op jit(solution)/shard_map/ppermute | solution.py:345
  7.0 3.7 %collective-permute-start.2 = (bf16[32,1408]{1,0:T(8,128)(2,1)S(1)}, bf16[32,1408]{1,0:T(8,128)(2,1)S(1)}, u32[]{:S(2)}, u32[]{:S(2)}) collective-permute-start(bf16[32,1408]{1,0:T(8,128)(2,1)S(1)} %get-tuple-element.26), channel_id=1, source_target_pairs={{0,3},{1,0},{2,1},{3,2},{4,7},{5,4},{6,5},{7,6},{8,11},{9,8},{10,9... | collective-permute-start | bytes 270344 | tf_op jit(solution)/shard_map/ppermute | solution.py:345
  11.4 6.3 %collective-permute-start.3 = (bf16[2,16,1408]{2,1,0:T(8,128)(2,1)S(1)}, bf16[2,16,1408]{2,1,0:T(8,128)(2,1)S(1)}, u32[]{:S(2)}, u32[]{:S(2)}) collective-permute-start(bf16[2,16,1408]{2,1,0:T(8,128)(2,1)S(1)} %get-tuple-element.30), channel_id=1, source_target_pairs={{0,2},{1,3},{2,0},{3,1},{4,6},{5,7},{6,4},{7,5},{8,10},{9,11},{10,... | collective-permute-start | bytes 270344 | tf_op jit(solution)/shard_map/ppermute | solution.py:345
  13.1 5.2 %collective-permute-start.4 = (bf16[2,16,1408]{2,1,0:T(8,128)(2,1)S(1)}, bf16[2,16,1408]{2,1,0:T(8,128)(2,1)S(1)}, u32[]{:S(2)}, u32[]{:S(2)}) collective-permute-start(bf16[2,16,1408]{2,1,0:T(8,128)(2,1)S(1)} %get-tuple-element.31), channel_id=1, source_target_pairs={{0,1},{1,2},{2,3},{3,0},{4,5},{5,6},{6,7},{7,4},{8,9},{9,10},{10,1... | collective-permute-start | bytes 270344 | tf_op jit(solution)/shard_map/ppermute | solution.py:345
  14.3 4.0 %collective-permute-start.5 = (bf16[2,16,1408]{2,1,0:T(8,128)(2,1)S(1)}, bf16[2,16,1408]{2,1,0:T(8,128)(2,1)S(1)}, u32[]{:S(2)}, u32[]{:S(2)}) collective-permute-start(bf16[2,16,1408]{2,1,0:T(8,128)(2,1)S(1)} %get-tuple-element.32), channel_id=1, source_target_pairs={{0,3},{1,0},{2,1},{3,2},{4,7},{5,4},{6,5},{7,6},{8,11},{9,8},{10,9... | collective-permute-start | bytes 270344 | tf_op jit(solution)/shard_map/ppermute | solution.py:345
